TPU v7x, 256 devices: a whole 4x4x8 slice. The times are simulated.
256 devices in a mesh: ent: 64 (over z, y, core), rel: 4 (over x).
Axes of the slice: x: 4, y: 4, z: 8, core: 2. Of those that a mesh axis runs over, the one named last changes fastest.
Arguments:
- entity_rows: bfloat16 [65536, 256], P('ent'), may hold values from -2.5 to 2.5
- request_rows: int32 [64, 64, 32], P('ent'), may hold values from 0 to 1023
- edge_heads: int32 [262144], P(('ent', 'rel')), may hold values from 0 to 1023
- edge_rels: int32 [262144], P(('ent', 'rel')), may hold values from 0 to 7
- edge_tails: int32 [262144], P(('ent', 'rel')), may hold values from 0 to 2047
- edge_counts: int32 [256], P(('ent', 'rel')), may hold values from 1 to 1024, 163840 in all
- negative_rows: int32 [65536], P(('ent', 'rel')), may hold values from 0 to 1023
- relation_blocks: bfloat16 [32, 8, 32, 32], P('rel'), may hold values from -1 to 1
Outputs:
- entity_grad: float32 [65536, 256], P('ent')
- relation_grad: float32 [32, 8, 32, 32], P('rel')
Inputs may be any that keep to these rules, and one draw needn't show every extreme that they name: Edge slots of bucket b at or past edge_counts[b] are ignored; some bucket is full in every draw.
All inputs are finite; a program needn't handle non-finite values. No bound on the sum of `edge_counts` on one device may be relied on, other than what follows from the above.
Results may differ from a plain program's by a relative error of at most 0.009.
Values may be sent and summed in bfloat16 or wider, within the bound.
No kernel may reach another device: no remote copies, remote signals or barrier semaphores. Data moves between devices by JAX's collectives and lax.ppermute only.
A program may use at most 64 MiB of HBM per device.

v0:
```python
import math

import jax
import jax.numpy as jnp
from jax import lax
from jax.sharding import PartitionSpec as P


def pick_rows(indices, source_table):
    row_total = indices.shape[0]
    block_size = math.gcd(row_total, 256)
    grouped = indices.reshape(row_total // block_size, block_size)
    columns = jnp.arange(source_table.shape[0], dtype=jnp.int32)

    def pick_block(index_block):
        one_hot = (index_block[:, None] == columns[None, :]).astype(jnp.bfloat16)
        return jnp.dot(one_hot, source_table, preferred_element_type=jnp.float32).astype(
            jnp.bfloat16
        )

    picked = lax.map(pick_block, grouped)
    return picked.reshape(row_total, source_table.shape[1])


def owner_add(indices, gradients, entity_count):
    start_value = jnp.zeros((entity_count, gradients.shape[1]), jnp.float32)
    return start_value.at[indices].add(gradients)


def local(
    entity_rows,
    request_rows,
    edge_heads,
    edge_rels,
    edge_tails,
    edge_counts,
    negative_rows,
    relation_blocks,
):
    entity_count, feature_width = entity_rows.shape
    part_count = request_rows.shape[1]
    slot_count = request_rows.shape[2]
    r_count, block_count, block_width = (
        relation_blocks.shape[0],
        relation_blocks.shape[1],
        relation_blocks.shape[2],
    )
    neg_count = negative_rows.shape[0]
    owner_lists = lax.all_to_all(request_rows, "ent", split_axis=1, concat_axis=0, tiled=True)
    wanted = pick_rows(owner_lists.reshape(-1), entity_rows).reshape(
        part_count, 1, slot_count, feature_width
    )
    fetched = lax.all_to_all(wanted, "ent", split_axis=0, concat_axis=1, tiled=True)
    fetched = fetched.reshape(part_count * slot_count, feature_width)
    neg_rows = pick_rows(negative_rows, entity_rows)
    edge_dev = edge_heads.shape[0]
    block_size = math.gcd(edge_dev, 256)
    block_total = edge_dev // block_size
    live_count = edge_counts[0]
    positions = jnp.arange(edge_dev, dtype=jnp.int32).reshape(block_total, block_size)
    entity_columns = jnp.arange(entity_count, dtype=jnp.int32)
    slot_columns = jnp.arange(part_count * slot_count, dtype=jnp.int32)
    rel_columns = jnp.arange(r_count, dtype=jnp.int32)
    contract_rows = (((0,), (0,)), ((), ()))

    def edge_block(running, block_inputs):
        slot_acc, entity_acc, neg_acc, relation_acc = running
        head_ids, rel_ids, tail_ids, places = block_inputs
        live_mask = (places < live_count).astype(jnp.float32)
        head_hot = (head_ids[:, None] == entity_columns[None, :]).astype(jnp.bfloat16)
        tail_hot = (tail_ids[:, None] == slot_columns[None, :]).astype(jnp.bfloat16)
        head_rows = jnp.dot(head_hot, entity_rows, preferred_element_type=jnp.float32).astype(
            jnp.bfloat16
        )
        tail_rows = jnp.dot(tail_hot, fetched, preferred_element_type=jnp.float32).astype(
            jnp.bfloat16
        )
        rel_hot = (rel_ids[:, None] == rel_columns[None, :]).astype(jnp.float32)
        head_split = head_rows.reshape(block_size, block_count, block_width)
        proj_all = jnp.einsum(
            "enb,rnbc->renc", head_split, relation_blocks, preferred_element_type=jnp.float32
        )
        projected = (
            jnp.sum(rel_hot.T[:, :, None, None] * proj_all, 0)
            .reshape(block_size, feature_width)
            .astype(jnp.bfloat16)
        )
        projected_wide = projected.astype(jnp.float32)
        positive = jnp.sum(projected_wide * tail_rows.astype(jnp.float32), -1)
        negative = lax.dot_general(
            projected, neg_rows, (((1,), (1,)), ((), ())), preferred_element_type=jnp.float32
        )
        pos_weight = -live_mask * jax.nn.sigmoid(-positive)
        neg_weight = (live_mask[:, None] * jax.nn.sigmoid(negative) / neg_count).astype(
            jnp.bfloat16
        )
        grad_proj = (
            pos_weight[:, None] * tail_rows.astype(jnp.float32)
            + jnp.dot(neg_weight, neg_rows, preferred_element_type=jnp.float32)
        ).astype(jnp.bfloat16)
        weighted = (pos_weight[:, None] * projected_wide).astype(jnp.bfloat16)
        grad_split = grad_proj.reshape(block_size, block_count, block_width)
        back_all = jnp.einsum(
            "enc,rnbc->renb", grad_split, relation_blocks, preferred_element_type=jnp.float32
        )
        head_grad = (
            jnp.sum(rel_hot.T[:, :, None, None] * back_all, 0)
            .reshape(block_size, feature_width)
            .astype(jnp.bfloat16)
        )
        slot_acc = slot_acc + lax.dot_general(
            tail_hot, weighted, contract_rows, preferred_element_type=jnp.float32
        )
        entity_acc = entity_acc + lax.dot_general(
            head_hot, head_grad, contract_rows, preferred_element_type=jnp.float32
        )
        neg_acc = neg_acc + lax.dot_general(
            neg_weight, projected, contract_rows, preferred_element_type=jnp.float32
        )
        masked_heads = rel_hot.T.astype(jnp.bfloat16)[:, :, None, None] * head_split[None]
        relation_acc = relation_acc + jnp.einsum(
            "renb,enc->rnbc", masked_heads, grad_split, preferred_element_type=jnp.float32
        )
        return ((slot_acc, entity_acc, neg_acc, relation_acc), None)

    start_values = (
        jnp.zeros((part_count * slot_count, feature_width), jnp.float32),
        jnp.zeros((entity_count, feature_width), jnp.float32),
        jnp.zeros((neg_count, feature_width), jnp.float32),
        jnp.zeros(relation_blocks.shape, jnp.float32),
    )
    block_inputs = (
        edge_heads.reshape(block_total, block_size),
        edge_rels.reshape(block_total, block_size),
        edge_tails.reshape(block_total, block_size),
        positions,
    )
    (slot_acc, entity_acc, neg_acc, relation_acc), _ = lax.scan(
        edge_block, start_values, block_inputs
    )
    neg_hot = (negative_rows[:, None] == entity_columns[None, :]).astype(jnp.bfloat16)
    entity_acc = entity_acc + lax.dot_general(
        neg_hot, neg_acc.astype(jnp.bfloat16), contract_rows, preferred_element_type=jnp.float32
    )
    slot_grads = slot_acc.reshape(1, part_count, slot_count, feature_width)
    returned = lax.all_to_all(
        slot_grads.astype(jnp.bfloat16), "ent", split_axis=1, concat_axis=0, tiled=True
    ).astype(slot_grads.dtype)
    entity_acc = entity_acc + owner_add(
        owner_lists.reshape(-1), returned.reshape(-1, feature_width), entity_count
    )
    entity_grad = lax.psum(entity_acc, "rel")
    relation_grad = lax.psum(relation_acc, "ent")
    return (entity_grad, relation_grad)


def solution(mesh):
    in_specs = (
        P("ent", None),
        P("ent", None, None),
        P(("ent", "rel")),
        P(("ent", "rel")),
        P(("ent", "rel")),
        P(("ent", "rel")),
        P(("ent", "rel")),
        P("rel", None, None, None),
    )
    out_specs = (P("ent", None), P("rel", None, None, None))
    return jax.shard_map(local, mesh=mesh, in_specs=in_specs, out_specs=out_specs, check_vma=False)
```

profile of v0, /device:TPU:1, one launch (start us, length us, event | category | flops | bytes accessed | tf_op | source)
XLA Modules:
  0.0 382.1 jit_solution(16212449031649504692)
XLA Ops:
  8.6 13.1 %all-to-all-start = ((s32[1,64,32]{2,0,1:T(1,128)}), s32[1,64,32]{2,0,1:T(1,128)S(1)}, u32[]{:S(2)}, u32[]{:S(2)}) async-start(s32[1,64,32]{2,0,1:T(1,128)} %copy.20), calls=%async_computation | async-start | bytes 65536 | tf_op jit(solution)/shard_map/all_to_all | solution.py:49
  21.7 9.3 %all-to-all-done = s32[1,64,32]{2,0,1:T(1,128)S(1)} async-done(((s32[1,64,32]{2,0,1:T(1,128)}), s32[1,64,32]{2,0,1:T(1,128)S(1)}, u32[]{:S(2)}, u32[]{:S(2)}) %all-to-all-start) | async-done | bytes 8224 | tf_op jit(solution)/shard_map/all_to_all | solution.py:49
  32.4 16.5 %while.32 = (s32[]{:T(128)}, bf16[8,256,256]{2,1,0:T(8,128)(2,1)}, s32[8,256]{1,0:T(8,128)S(1)}, bf16[1024,256]{1,0:T(8,128)(2,1)}, s32[]{:T(128)}) while((s32[]{:T(128)}, bf16[8,256,256]{2,1,0:T(8,128)(2,1)}, s32[8,256]{1,0:T(8,128)S(1)}, bf16[1024,256]{1,0:T(8,128)(2,1)}, s32[]{:T(128)}) %tuple.56), condition=%wide.region_1.2_spmd.clone, body=%wide.region_0.1_spmd.clone.sunk | while | flops 134545408 | bytes 658509 | solution.py:21
  32.4 2.1 fusion.90
  34.5 2.1 fusion.90
  36.5 2.1 fusion.90
  38.6 2.1 fusion.90
  40.6 2.0 fusion.90
  42.7 2.0 fusion.90
  44.8 2.1 fusion.90
  46.8 2.1 fusion.90
  48.9 5.7 %all-to-all-start.1 = ((bf16[64,1,32,256]{3,2,1,0:T(8,128)(2,1)}), bf16[64,1,32,256]{3,2,1,0:T(8,128)(2,1)}, u32[]{:S(2)}, u32[]{:S(2)}) async-start(bf16[64,1,32,256]{3,2,1,0:T(8,128)(2,1)} %bitcast.1), calls=%async_computation.1 | async-start | bytes 2097152 | tf_op jit(solution)/shard_map/all_to_all | solution.py:53
  58.0 24.8 %all-to-all-done.1 = bf16[64,1,32,256]{3,2,1,0:T(8,128)(2,1)} async-done(((bf16[64,1,32,256]{3,2,1,0:T(8,128)(2,1)}), bf16[64,1,32,256]{3,2,1,0:T(8,128)(2,1)}, u32[]{:S(2)}, u32[]{:S(2)}) %all-to-all-start.1) | async-done | bytes 1048608 | tf_op jit(solution)/shard_map/all_to_all | solution.py:53
  82.8 38.9 %while.33 = (s32[]{:T(128)}, f32[2048,256]{1,0:T(8,128)S(1)}, f32[1024,256]{1,0:T(8,128)S(1)}, f32[256,256]{1,0:T(8,128)S(1)}, f32[8,8,32,32]{2,3,0,1:T(8,128)},...) while((s32[]{:T(128)}, f32[2048,256]{1,0:T(8,128)S(1)}, ...), condition=%wide.region_6.7_spmd.clone, body=%wide.region_2.6_spmd.clone.sunk | while | flops 1016077568 | bytes 14733582 | solution.py:138
  87.1 2.1 fusion.111
  96.8 2.1 fusion.111
  106.6 2.1 fusion.111
  116.3 2.1 fusion.111
  122.8 6.4 %all-to-all-start.2 = ((bf16[1,64,32,256]{3,2,0,1:T(8,128)(2,1)}), bf16[1,64,32,256]{3,2,0,1:T(8,128)(2,1)S(1)}, u32[]{:S(2)}, u32[]{:S(2)}) async-start(bf16[1,64,32,256]{3,2,0,1:T(8,128)(2,1)} %bitcast.124), calls=%async_computation.2 | async-start | bytes 2097152 | tf_op jit(solution)/shard_map/all_to_all | solution.py:146
  131.4 26.8 %all-to-all-done.2 = bf16[1,64,32,256]{3,2,0,1:T(8,128)(2,1)S(1)} async-done(((bf16[1,64,32,256]{3,2,0,1:T(8,128)(2,1)}), bf16[1,64,32,256]{3,2,0,1:T(8,128)(2,1)S(1)}, u32[]{:S(2)}, u32[]{:S(2)}) %all-to-all-start.2) | async-done | bytes 1048608 | tf_op jit(solution)/shard_map/all_to_all | solution.py:146
  158.2 12.0 %scatter_custom_fusion = f32[1024,256]{1,0:T(8,128)S(1)} fusion(f32[1024,256]{1,0:T(8,128)S(1)} %convolution_add_fusion.4, s32[2048]{0:T(1024)S(1)} %bitcast.138, bf16[2048,256]{1,0:T(8,128)(2,1)S(1)} %bitcast.125), kind=kCustom, calls=%fused_computation.57 | custom fusion | flops 1048576 | bytes 2097152 | tf_op jit(solution)/shard_map/scatter-add | solution.py:27
  171.2 149.3 %all-reduce.5.cloned.1.call-done = f32[8,8,32,32]{3,2,1,0:T(8,128)} async-done(((f32[8,8,32,32]{3,2,1,0:T(8,128)}), f32[8,8,32,32]{3,2,1,0:T(8,128)}) %all-reduce.5.cloned.1.call-update) | async-done | bytes 262160 | tf_op jit(solution)/shard_map/psum | solution.py:153
  320.5 51.6 %all-reduce.3.cloned.1.call-done = f32[1024,256]{1,0:T(8,128)} async-done(((f32[1024,256]{1,0:T(8,128)}), f32[1024,256]{1,0:T(8,128)}) %all-reduce.3.cloned.1.call-update) | async-done | bytes 1048592 | tf_op jit(solution)/shard_map/psum | solution.py:152
  372.1 2.3 copy.51
  (131 shorter events, 41.3 us)
Async XLA Ops:
  8.6 22.5 %all-to-all-start = ((s32[1,64,32]{2,0,1:T(1,128)}), s32[1,64,32]{2,0,1:T(1,128)S(1)}, u32[]{:S(2)}, u32[]{:S(2)}) async-start(s32[1,64,32]{2,0,1:T(1,128)} %copy.20), calls=%async_computation | async-start | bytes 65536 | tf_op jit(solution)/shard_map/all_to_all | solution.py:49
  48.9 5.7 %copy-start.8 = (s32[1024]{0:T(1024)S(1)}, s32[1024]{0:T(1024)}, u32[]{:S(2)}) copy-start(s32[1024]{0:T(1024)} %param.14) | copy-start | bytes 12292
  48.9 5.8 %copy-start.9 = (s32[1024]{0:T(1024)S(1)}, s32[1024]{0:T(1024)}, u32[]{:S(2)}) copy-start(s32[1024]{0:T(1024)} %param.15) | copy-start | bytes 12292
  48.9 5.8 %copy-start.10 = (s32[1024]{0:T(1024)S(1)}, s32[1024]{0:T(1024)}, u32[]{:S(2)}) copy-start(s32[1024]{0:T(1024)} %param.16) | copy-start | bytes 12292
  48.9 33.9 %all-to-all-start.1 = ((bf16[64,1,32,256]{3,2,1,0:T(8,128)(2,1)}), bf16[64,1,32,256]{3,2,1,0:T(8,128)(2,1)}, u32[]{:S(2)}, u32[]{:S(2)}) async-start(bf16[64,1,32,256]{3,2,1,0:T(8,128)(2,1)} %bitcast.1), calls=%async_computation.1 | async-start | bytes 2097152 | tf_op jit(solution)/shard_map/all_to_all | solution.py:53
  86.8 2.6 copy-start.5
  87.1 2.8 copy-start
  90.8 1.7 copy-start.1
  96.6 2.6 copy-start.5
  96.8 2.8 copy-start
  100.6 1.7 copy-start.1
  106.3 2.6 copy-start.5
  106.6 2.8 copy-start
  110.3 1.7 copy-start.1
  116.0 2.6 copy-start.5
  116.3 2.8 copy-start
  120.0 1.7 copy-start.1
  121.7 7.6 %copy-start.7 = (s32[1,64,32]{2,0,1:T(1,128)S(1)}, s32[1,64,32]{2,0,1:T(1,128)}, u32[]{:S(2)}) copy-start(s32[1,64,32]{2,0,1:T(1,128)} %copy-done.6) | copy-start | bytes 24580
  122.8 6.6 %copy-start.2 = (f32[8,8,32,32]{2,3,0,1:T(8,128)S(1)}, f32[8,8,32,32]{2,3,0,1:T(8,128)}, u32[]{:S(2)}) copy-start(f32[8,8,32,32]{2,3,0,1:T(8,128)} %get-tuple-element.138) | copy-start | bytes 786436
  122.8 35.4 %all-to-all-start.2 = ((bf16[1,64,32,256]{3,2,0,1:T(8,128)(2,1)}), bf16[1,64,32,256]{3,2,0,1:T(8,128)(2,1)S(1)}, u32[]{:S(2)}, u32[]{:S(2)}) async-start(bf16[1,64,32,256]{3,2,0,1:T(8,128)(2,1)} %bitcast.124), calls=%async_computation.2 | async-start | bytes 2097152 | tf_op jit(solution)/shard_map/all_to_all | solution.py:146
  129.2 1.6 copy-start.11
  129.2 191.2 %all-reduce.5.cloned.1.call-start = ((), (), s32[]{:S(2)}) async-start(), calls=%async_computation.4 | async-start | bytes 2097152 | tf_op jit(solution)/shard_map/psum | solution.py:153
  130.8 241.3 %all-reduce.3.cloned.1.call-start = ((), (), s32[]{:S(2)}) async-start(), calls=%async_computation.3 | async-start | bytes 2097152 | tf_op jit(solution)/shard_map/psum | solution.py:152
  320.5 53.9 %copy-start.4 = (f32[8,8,32,32]{3,2,1,0:T(8,128)S(1)}, f32[8,8,32,32]{3,2,1,0:T(8,128)}, u32[]{:S(2)}) copy-start(f32[8,8,32,32]{3,2,1,0:T(8,128)} %all-reduce.5.cloned.1.call-done) | copy-start | bytes 786436
  (2 other events, 2.3 us)
Sparse Core Ops, SparseCore 0:
  133.5 186.9 all-reduce.4
  323.4 48.6 all-reduce.2
where the time goes:
time: 384 us; the launch traced here: 382 us
  waiting for transfers between devices  262 us (68%)
  matrix products  53.8 us (14%)
  starting transfers between devices  25.3 us (7%)
  other arithmetic  16.5 us (4%)
  between operations  14.2 us (4%)
  local copies, waits for them, and re-layouts  9.81 us (3%)
    psum x1, waiting for transfers between devices, local(): relation_grad = lax.psum(relation_acc, 'ent')  149 us
    psum x1, waiting for transfers between devices, local(): entity_grad = lax.psum(entity_acc, 'rel')  51.6 us
    all_to_all x1, waiting for transfers between devices, local(): lax.all_to_all(slot_grads.astype(jnp.bfloat16), 'ent', split_axis=1, conc...  26.8 us
    all_to_all x1, waiting for transfers between devices, local(): lax.all_to_all(wanted, 'ent', split_axis=0, concat_axis=1, tiled=True)  24.8 us
    dot_general x9, matrix products, pick_block(): jnp.dot(one_hot, source_table, preferred_element_type=jnp.float32)  17.8 us
    all_to_all x1, starting transfers between devices, local(): lax.all_to_all(request_rows, 'ent', split_axis=1, concat_axis=0, tiled=True)  13.1 us
    scatter-add x1, other arithmetic, owner_add(): return start_value.at[indices].add(gradients)  12 us
    all_to_all x1, waiting for transfers between devices, local(): lax.all_to_all(request_rows, 'ent', split_axis=1, concat_axis=0, tiled=True)  9.32 us
  transfers between devices with their start and end apart: 5, of which 5 were waited for; matrix products, arithmetic and copies ran while one was open for 5% of the time, Pallas kernels for 0%

commit v1 on v0

v1 whole, which is shorter than its diff:
```python
import functools

import jax
import jax.numpy as jnp
from jax import lax
from jax.experimental import pallas as pl
from jax.experimental.pallas import tpu as pltpu
from jax.sharding import PartitionSpec as P

F32 = jnp.float32
BF16 = jnp.bfloat16
TILE = 256
SMEM = pl.BlockSpec(memory_space=pltpu.SMEM)
CONTRACT_LAST = (((1,), (1,)), ((), ()))


def iota(shape, axis):
    return lax.broadcasted_iota(jnp.int32, shape, axis)


def dot(a, b):
    return jnp.dot(a, b, preferred_element_type=F32)


def column(row):
    eye = iota((128, 128), 0) == iota((128, 128), 1)
    parts = []
    for k in range(row.shape[1] // 128):
        wide = jnp.broadcast_to(row[:, k * 128 : (k + 1) * 128].astype(F32), (128, 128))
        parts.append(jnp.sum(jnp.where(eye, wide, 0.0), axis=1, keepdims=True))
    return jnp.concatenate(parts, axis=0).astype(jnp.int32)


def hot_rows(col, width):
    return jnp.where(col == iota((col.shape[0], width), 1), 1.0, 0.0).astype(BF16)


def hot_columns(row, height):
    return jnp.where(row == iota((height, row.shape[1]), 0), 1.0, 0.0).astype(BF16)


def whole(shape):
    return pl.BlockSpec(shape, lambda *_: (0,) * len(shape))


def params(steps=1):
    return pltpu.CompilerParams(
        dimension_semantics=("arbitrary",) * (1 if steps else 0),
        vmem_limit_bytes=48 * 1024 * 1024,
    )


def cost(flops, nbytes):
    return pl.CostEstimate(flops=int(flops), bytes_accessed=int(nbytes), transcendentals=0)


def pick_kernel(share, scal, lists, table, out):
    n = lists.shape[0]
    wide = jnp.broadcast_to(lists[...].astype(F32)[:, None, :], (n, share, 128))
    wide = wide.reshape(n * share, 128)
    shape = (n * share, 128)
    wanted = iota(shape, 1) == scal[0] * share + iota(shape, 0) % share
    col = jnp.sum(jnp.where(wanted, wide, 0.0), axis=1, keepdims=True).astype(jnp.int32)
    out[...] = dot(hot_rows(col, table.shape[0]), table[...]).astype(BF16)


def rows_kernel(share, rels, scal, lists, out):
    n = lists.shape[0]
    wide = n * share
    ids = jnp.concatenate([lists[...], jnp.zeros((128 - n, 128), jnp.int32)], axis=0)
    turned = ids.astype(F32).T.astype(jnp.int32)
    spread = jnp.where(iota((128, wide), 1) // share == iota((128, wide), 0), 1.0, 0.0)
    spread = spread.astype(BF16)
    low = dot((turned & 31).astype(F32).astype(BF16), spread)
    high = dot((turned >> 5).astype(F32).astype(BF16), spread)
    value = high * 32.0 + low
    slot = iota((128, wide), 0)
    for c in range(rels):
        q = (scal[0] + c) % rels
        wanted = slot == q * share + iota((128, wide), 1) % share
        out[c : c + 1, :] = jnp.sum(jnp.where(wanted, value, 0.0), axis=0, keepdims=True).astype(
            jnp.int32
        )


def head_kernel(
    r_count, blocks, scal, heads, rels, negs, table, ops,
    proj_out, negpart_out, turned_out, nege_out, bd_out, neg_rows, neg_acc,
):
    step = pl.program_id(0)
    d = table.shape[1]
    width = d // blocks
    n_neg = neg_rows.shape[0]

    @pl.when(step == 0)
    def _():
        spread = jnp.where(iota((width, d), 1) % width == iota((width, d), 0), 1.0, 0.0)
        spread = spread.astype(BF16)
        inside = iota((d, d), 0) // width == iota((d, d), 1) // width
        for r in range(r_count):
            full = dot(ops[r * d : (r + 1) * d, :], spread)
            bd_out[r * d : (r + 1) * d, :] = jnp.where(inside, full, 0.0).astype(BF16)
        neg_hot = hot_rows(column(negs[...]), table.shape[0])
        neg_rows[...] = dot(neg_hot, table[...]).astype(BF16)
        neg_acc[...] = jnp.zeros_like(neg_acc)

    head_wide = dot(hot_rows(column(heads[0]), table.shape[0]), table[...])
    head = head_wide.astype(BF16)
    turned_out[...] = head_wide.T.astype(BF16)
    rel_col = column(rels[0])
    proj = jnp.zeros((TILE, d), F32)
    for r in range(r_count):
        masked = jnp.where(rel_col == r, head_wide, 0.0).astype(BF16)
        proj = proj + dot(masked, bd_out[r * d : (r + 1) * d, :])
    proj = proj.astype(BF16)
    proj_out[...] = proj
    negative = lax.dot_general(proj, neg_rows[...], CONTRACT_LAST, preferred_element_type=F32)
    live = step * TILE + iota((TILE, n_neg), 0) < scal[1]
    weight = jnp.where(live, jax.nn.sigmoid(negative) / n_neg, 0.0)
    negpart_out[...] = dot(weight.astype(BF16), neg_rows[...])
    neg_acc[...] += dot(weight.T.astype(BF16), proj)

    @pl.when(step == pl.num_programs(0) - 1)
    def _():
        grads = neg_acc[...].astype(BF16)
        for k in range(table.shape[0] // TILE):
            hot = hot_columns(negs[...] - k * TILE, TILE)
            nege_out[k * TILE : (k + 1) * TILE, :] = dot(hot, grads)


def tail_kernel(n_rel, share, scal, tails, proj, negpart, *refs):
    chunks, (gp_out, *outs), (weighted, places) = (
        refs[:n_rel], refs[n_rel : 2 * n_rel + 1], refs[2 * n_rel + 1 :],
    )
    step = pl.program_id(0)
    edges = pl.num_programs(0) * TILE
    rows = chunks[0].shape[0]
    slots = share * n_rel
    t = tails[0]
    slot = t % slots
    place = (slot // share - scal[0] + n_rel) % n_rel * rows
    place = place + t // slots * share + slot % share
    places[:, pl.ds(pl.multiple_of(step * TILE, TILE), TILE)] = place
    col = column(place)
    tail = jnp.zeros((TILE, proj.shape[1]), F32)
    for c in range(n_rel):
        tail = tail + dot(hot_rows(col - c * rows, rows), chunks[c][...])
    wide = proj[...].astype(F32)
    positive = jnp.sum(wide * tail, axis=1, keepdims=True)
    live = step * TILE + iota((TILE, 1), 0) < scal[1]
    pos_weight = jnp.where(live, -jax.nn.sigmoid(-positive), 0.0)
    gp_out[...] = (pos_weight * tail + negpart[...]).astype(BF16)
    weighted[pl.ds(pl.multiple_of(step * TILE, TILE), TILE), :] = (pos_weight * wide).astype(BF16)

    @pl.when(step == pl.num_programs(0) - 1)
    def _():
        for c in range(n_rel):
            for k in range(rows // TILE):
                hot = hot_columns(places[...] - (c * rows + k * TILE), TILE)
                outs[c][k * TILE : (k + 1) * TILE, :] = dot(hot, weighted[...]).astype(BF16)


def grad_kernel(
    blocks, n_rel, scal, heads, rels, gp, turned, nege, bd,
    rel_out, *refs,
):
    outs, (head_acc, rows_acc) = refs[:n_rel], refs[n_rel:]
    step = pl.program_id(0)
    edges, d = gp.shape
    width = d // blocks
    rel_row = rels[...]
    grads = gp[...]

    @pl.when(step == 0)
    def _():
        head_acc[...] = jnp.zeros_like(head_acc)

    masked = jnp.where(rel_row == step, turned[...].astype(F32), 0.0).astype(BF16)
    outer = dot(masked, grads)
    inside = iota((d, d), 0) // width == iota((d, d), 1) // width
    outer = jnp.where(inside, outer, 0.0)
    packed = outer[:width]
    for n in range(1, blocks):
        packed = packed + outer[n * width : (n + 1) * width]
    for half in range(d // 128):
        start = pl.multiple_of((half * pl.num_programs(0) + step) * width, width)
        rel_out[pl.ds(start, width), :] = packed[:, half * 128 : (half + 1) * 128].astype(BF16)
    for k in range(edges // TILE):
        part = pl.ds(k * TILE, TILE)
        rel_col = column(rel_row[:, k * TILE : (k + 1) * TILE])
        mine = jnp.where(rel_col == step, gp[part, :].astype(F32), 0.0).astype(BF16)
        head_acc[part, :] += lax.dot_general(mine, bd[...], CONTRACT_LAST, preferred_element_type=F32)

    @pl.when(step == pl.num_programs(0) - 1)
    def _():
        rows = nege.shape[0] // n_rel
        head_grad = head_acc[...].astype(BF16)
        for k in range(nege.shape[0] // TILE):
            part = slice(k * TILE, (k + 1) * TILE)
            rows_acc[part, :] = nege[part, :] + dot(hot_columns(heads[...] - k * TILE, TILE), head_grad)
        for c in range(n_rel):
            start = pl.multiple_of((scal[0] + c) % n_rel * rows, rows)
            outs[c][...] = rows_acc[pl.ds(start, rows), :].astype(BF16)


def owner_kernel(n_rel, scal, ids, *refs):
    slots, terms, out = refs[:n_rel], refs[n_rel : 2 * n_rel], refs[2 * n_rel]
    step = pl.program_id(0)
    rows = out.shape[0]
    total = jnp.zeros(out.shape, F32)
    for c in range(n_rel):
        total = total + dot(hot_columns(ids[c : c + 1, :] - step * rows, rows), slots[c][...])
    for c in range(n_rel):
        @pl.when((scal[0] + c) % n_rel == step)
        def _(c=c):
            out[...] = total + terms[c][...].astype(F32)


def relation_kernel(r_count, blocks, width, x, out):
    per = 128 // width
    for r in range(r_count):
        for n in range(blocks):
            start = (n // per * r_count + r) * width
            block = x[start : start + width, n % per * width : (n % per + 1) * width]
            out[r, n] = block.astype(F32)


def ring(x, n_rel, shift):
    return lax.ppermute(x, "rel", [((k + shift) % n_rel, k) for k in range(n_rel)])


def local(
    entity_rows, request_rows, edge_heads, edge_rels, edge_tails, edge_counts, negative_rows,
    relation_blocks,
):
    rows, d = entity_rows.shape
    parts, slots = request_rows.shape[1:]
    r_count, blocks, width = relation_blocks.shape[:3]
    edges, n_neg = edge_heads.shape[0], negative_rows.shape[0]
    n_rel = lax.axis_size("rel")
    share = slots // n_rel
    held = parts * share
    steps = edges // TILE
    me = lax.axis_index("rel").astype(jnp.int32)
    scal = jnp.concatenate([me.reshape(1), edge_counts])
    shaped = jax.ShapeDtypeStruct

    wide_lists = jnp.pad(request_rows.reshape(parts, slots), ((0, 0), (0, 128 - slots)))
    lists = lax.all_to_all(wide_lists, "ent", 0, 0, tiled=True)

    heads = edge_heads.reshape(steps, 1, TILE)
    rels = edge_rels.reshape(steps, 1, TILE)
    tails = edge_tails.reshape(steps, 1, TILE)
    negs = negative_rows.reshape(1, n_neg)
    id_block = pl.BlockSpec((1, 1, TILE), lambda i: (i, 0, 0))
    edge_block = pl.BlockSpec((TILE, d), lambda i: (i, 0))

    proj, negpart, turned, nege, bd = pl.pallas_call(
        functools.partial(head_kernel, r_count, blocks),
        grid=(steps,),
        in_specs=[
            SMEM, id_block, id_block, whole((1, n_neg)), whole((rows, d)),
            whole((r_count * d, width)),
        ],
        out_specs=[
            edge_block, edge_block, pl.BlockSpec((d, TILE), lambda i: (0, i)), whole((rows, d)),
            whole((r_count * d, d)),
        ],
        out_shape=[
            shaped((edges, d), BF16), shaped((edges, d), F32), shaped((d, edges), BF16),
            shaped((rows, d), F32), shaped((r_count * d, d), BF16),
        ],
        scratch_shapes=[pltpu.VMEM((n_neg, d), BF16), pltpu.VMEM((n_neg, d), F32)],
        compiler_params=params(),
        cost_estimate=cost(3e9, 6e6),
        name="head_step",
    )(scal, heads, rels, negs, entity_rows, relation_blocks.reshape(r_count * d, width))

    picked = pl.pallas_call(
        functools.partial(pick_kernel, share),
        in_specs=[SMEM, whole((parts, 128)), whole((rows, d))],
        out_specs=whole((held, d)),
        out_shape=shaped((held, d), BF16),
        compiler_params=params(0),
        cost_estimate=cost(2 * held * rows * d, 1e6),
        name="pick",
    )(scal, lists, entity_rows)
    list_rows = pl.pallas_call(
        functools.partial(rows_kernel, share, n_rel),
        in_specs=[SMEM, whole((parts, 128))],
        out_specs=whole((n_rel, held)),
        out_shape=shaped((n_rel, held), jnp.int32),
        compiler_params=params(0),
        cost_estimate=cost(1e8, 1e5),
        name="list_rows",
    )(scal, lists)

    fetched = [lax.all_to_all(picked, "ent", 0, 0, tiled=True)]
    fetched += [ring(fetched[0], n_rel, c) for c in range(1, n_rel)]

    grad_proj, *slot_parts = pl.pallas_call(
        functools.partial(tail_kernel, n_rel, share),
        grid=(steps,),
        in_specs=[SMEM, id_block, edge_block, edge_block] + [whole((held, d))] * n_rel,
        out_specs=[edge_block] + [whole((held, d))] * n_rel,
        out_shape=[shaped((edges, d), BF16)] + [shaped((held, d), BF16)] * n_rel,
        scratch_shapes=[pltpu.VMEM((edges, d), BF16), pltpu.VMEM((1, edges), jnp.int32)],
        compiler_params=params(),
        cost_estimate=cost(3e9, 5e6),
        name="tail_step",
    )(scal, tails, proj, negpart, *fetched)
    slot_sum = slot_parts[0].astype(F32)
    for c in range(1, n_rel):
        slot_sum = slot_sum + ring(slot_parts[c], n_rel, n_rel - c).astype(F32)

    rel_part, *row_parts = pl.pallas_call(
        functools.partial(grad_kernel, blocks, n_rel),
        grid=(r_count,),
        in_specs=[
            SMEM, whole((1, edges)), whole((1, edges)), whole((edges, d)), whole((d, edges)),
            whole((rows, d)), pl.BlockSpec((d, d), lambda r: (r, 0)),
        ],
        out_specs=[whole((r_count * width * d // 128, 128))] + [whole((rows // n_rel, d))] * n_rel,
        out_shape=[shaped((r_count * width * d // 128, 128), BF16)]
        + [shaped((rows // n_rel, d), BF16)] * n_rel,
        scratch_shapes=[pltpu.VMEM((edges, d), F32), pltpu.VMEM((rows, d), F32)],
        compiler_params=params(),
        cost_estimate=cost(3e9, 6e6),
        name="grad_step",
    )(scal, edge_heads.reshape(1, edges), edge_rels.reshape(1, edges), grad_proj, turned, nege, bd)

    packed = jnp.concatenate([slot_sum.astype(BF16), rel_part], axis=1)
    returned = lax.all_to_all(packed, "ent", 0, 0, tiled=True)
    slot_back = [returned[:, :d]]
    slot_back += [ring(slot_back[0], n_rel, c) for c in range(1, n_rel)]
    rel_sum = jnp.sum(returned[:, d:].reshape(parts, -1, 128).astype(F32), 0).astype(BF16)
    rel_all = jnp.broadcast_to(rel_sum[None], (parts,) + rel_sum.shape).reshape(-1, 128)
    rel_all = lax.all_to_all(rel_all, "ent", 0, 0, tiled=True)

    row_sum = row_parts[0].astype(F32)
    for c in range(1, n_rel):
        row_sum = row_sum + ring(row_parts[c], n_rel, n_rel - c).astype(F32)
    row_terms = [row_sum.astype(BF16)]
    row_terms += [ring(row_terms[0], n_rel, c) for c in range(1, n_rel)]

    entity_grad = pl.pallas_call(
        functools.partial(owner_kernel, n_rel),
        grid=(n_rel,),
        in_specs=[SMEM, whole((n_rel, held))]
        + [whole((held, d))] * n_rel
        + [whole((rows // n_rel, d))] * n_rel,
        out_specs=pl.BlockSpec((rows // n_rel, d), lambda q: (q, 0)),
        out_shape=shaped((rows, d), F32),
        compiler_params=params(),
        cost_estimate=cost(1e9, 3e6),
        name="owner_add",
    )(scal, list_rows, *slot_back, *row_terms)
    relation_grad = pl.pallas_call(
        functools.partial(relation_kernel, r_count, blocks, width),
        in_specs=[whole(rel_all.shape)],
        out_specs=whole(relation_blocks.shape),
        out_shape=shaped(relation_blocks.shape, F32),
        compiler_params=params(0),
        cost_estimate=cost(1e6, 1.2e6),
        name="relation_out",
    )(rel_all)
    return entity_grad, relation_grad


def solution(mesh):
    in_specs = (
        P("ent", None),
        P("ent", None, None),
        P(("ent", "rel")),
        P(("ent", "rel")),
        P(("ent", "rel")),
        P(("ent", "rel")),
        P(("ent", "rel")),
        P("rel", None, None, None),
    )
    out_specs = (P("ent", None), P("rel", None, None, None))
    return jax.shard_map(local, mesh=mesh, in_specs=in_specs, out_specs=out_specs, check_vma=False)
```

time: 384 us -> 131 us (0.34)
  waiting for transfers between devices: 262 us -> 31.6 us
  matrix products: 53.8 us -> 0 us
  Pallas kernels: 0 us -> 27 us
  starting transfers between devices: 25.3 us -> 48 us
  blocking collectives: 0 us -> 17.1 us
  other arithmetic: 16.5 us -> 1.14 us
  between operations: 14.2 us -> 1.43 us
  local copies, waits for them, and re-layouts: 9.81 us -> 3.84 us
    psum x2 -> x0, waiting for transfers between devices: 201 us -> none  [the longest x1 149 us: local(): relation_grad = lax.psum(relation_acc, 'ent')]
    dot_general x50 -> x0, matrix products: 53.8 us -> none  [the longest x9 17.8 us: pick_block(): jnp.dot(one_hot, source_table, preferred_element_type=jnp.float32)]
    all_to_all x3, waiting for transfers between devices: 60.9 us -> 20.8 us  [the longest x1 8.6 us: local(): lists = lax.all_to_all(wide_lists, 'ent', 0, 0, tiled=True)]
    pallas_call x0 -> x7, Pallas kernels: none -> 27 us  [the longest x1 7.85 us: local(): pl.pallas_call(functools.partial(head_kernel, r_count, blocks), grid=(ste...]
    ppermute x0 -> x15, starting transfers between devices: none -> 20.8 us  [ring(): lax.ppermute(x, 'rel', [((k + shift) % n_rel, k) for k in range(n_rel)])]
    all_to_all x0 -> x1, blocking collectives: none -> 17.1 us  [local(): fetched = [lax.all_to_all(picked, 'ent', 0, 0, tiled=True)]]
    scatter-add x1 -> x0, other arithmetic: 12 us -> none  [owner_add(): return start_value.at[indices].add(gradients)]
    ppermute x0 -> x15, waiting for transfers between devices: none -> 10.8 us  [ring(): lax.ppermute(x, 'rel', [((k + shift) % n_rel, k) for k in range(n_rel)])]
  transfers between devices with their start and end apart: 5 -> 18, of which waited for: 5 -> 7; matrix products, arithmetic and copies ran while one was open for 5% -> 1% of each run, Pallas kernels for 0% -> 13%
where the time goes in v1:
time: 131 us; the launch traced here: 130 us
  starting transfers between devices  48 us (37%)
  waiting for transfers between devices  31.6 us (24%)
  Pallas kernels  27 us (21%)
  blocking collectives  17.1 us (13%)
  local copies, waits for them, and re-layouts  3.84 us (3%)
  between operations  1.43 us (1%)
    ppermute x15, starting transfers between devices, ring(): lax.ppermute(x, 'rel', [((k + shift) % n_rel, k) for k in range(n_rel)])  20.8 us
    all_to_all x1, blocking collectives, local(): fetched = [lax.all_to_all(picked, 'ent', 0, 0, tiled=True)]  17.1 us
    all_to_all x1, starting transfers between devices, local(): lists = lax.all_to_all(wide_lists, 'ent', 0, 0, tiled=True)  13.1 us
    ppermute x15, waiting for transfers between devices, ring(): lax.ppermute(x, 'rel', [((k + shift) % n_rel, k) for k in range(n_rel)])  10.8 us
    all_to_all x1, waiting for transfers between devices, local(): lists = lax.all_to_all(wide_lists, 'ent', 0, 0, tiled=True)  8.6 us
    all_to_all x1, starting transfers between devices, local(): rel_all = lax.all_to_all(rel_all, 'ent', 0, 0, tiled=True)  8.49 us
    all_to_all x1, waiting for transfers between devices, local(): rel_all = lax.all_to_all(rel_all, 'ent', 0, 0, tiled=True)  7.96 us
    pallas_call x1, Pallas kernels, local(): pl.pallas_call(functools.partial(head_kernel, r_count, blocks), grid=(ste...  7.85 us
  transfers between devices with their start and end apart: 18, of which 7 were waited for; matrix products, arithmetic and copies ran while one was open for 1% of the time, Pallas kernels for 13%

profile of v1, /device:TPU:1, one launch (start us, length us, event | category | flops | bytes accessed | tf_op | source)
XLA Modules:
  0.0 130.1 jit_solution(17191985961453124919)
XLA Ops:
  2.1 13.1 %all-to-all-start = ((s32[64,1,128]{2,1,0:T(1,128)}), s32[64,1,128]{2,1,0:T(1,128)S(1)}, u32[]{:S(2)}, u32[]{:S(2)}) async-start(s32[64,1,128]{2,1,0:T(1,128)} %bitcast.2), calls=%async_computation | async-start | bytes 65536 | tf_op jit(solution)/shard_map/all_to_all | solution.py:249
  15.9 8.6 %all-to-all-done = s32[64,1,128]{2,1,0:T(1,128)S(1)} async-done(((s32[64,1,128]{2,1,0:T(1,128)}), s32[64,1,128]{2,1,0:T(1,128)S(1)}, u32[]{:S(2)}, u32[]{:S(2)}) %all-to-all-start) | async-done | bytes 32800 | tf_op jit(solution)/shard_map/all_to_all | solution.py:249
  26.7 17.1 %all_to_all.42 = bf16[64,8,256]{2,1,0:T(8,128)(2,1)S(1)} all-to-all(bf16[64,8,256]{2,1,0:T(8,128)(2,1)S(1)} %bitcast.26), channel_id=1, replica_groups=mesh['ent'=64,'rel'=4] {'ent'}, dimensions={0} | all-to-all | bytes 524288 | tf_op jit(solution)/shard_map/all_to_all | solution.py:298
  43.7 1.2 collective-permute-start.2
  45.0 2.4 %collective-permute-start.1 = (bf16[512,256]{1,0:T(8,128)(2,1)S(1)}, bf16[512,256]{1,0:T(8,128)(2,1)S(1)}, u32[]{:S(2)}, u32[]{:S(2)}) collective-permute-start(bf16[512,256]{1,0:T(8,128)(2,1)S(1)} %bitcast.23), channel_id=1, source_target_pairs={{2,0},{3,1},{0,2},{1,3},{6,4},{7,5},{4,6},{5,7},{10,8},{11,9},{8,1... | collective-permute-start | bytes 786440 | tf_op jit(solution)/shard_map/ppermute | solution.py:229
  47.4 1.2 collective-permute-start
  49.2 7.8 %head_step.1 = (bf16[1024,256]{1,0:T(8,128)(2,1)S(1)}, f32[1024,256]{1,0:T(8,128)S(1)}, bf16[256,1024]{1,0:T(8,128)(2,1)S(1)}, f32[1024,256]{1,0:T(8,128)S(1)}, bf16[2048,256]{1,0:T(8,128)(2,1)S(1)}) custom-call(s32[2]{0:T(128)S(1)} %pad_add_fusion.scal, s32[4,1,256]{2,1,0:T(1,128)S(1)} %bitcast.31, s32[4,1,256]{2,1,0:T(1,128)S(1)} %bitcast.33, ...), custom_call_target="tpu_custom_call" | custom-call | flops 3000000000 | bytes 6000000 | tf_op jit(solution)/shard_map/head_step/pallas_call | solution.py:258
  57.1 2.0 %collective-permute-done.1.refs_2_ = bf16[512,256]{1,0:T(8,128)(2,1)S(1)} collective-permute-done((bf16[512,256]{1,0:T(8,128)(2,1)S(1)}, bf16[512,256]{1,0:T(8,128)(2,1)S(1)}, u32[]{:S(2)}, u32[]{:S(2)}) %collective-permute-start.1) | collective-permute-done | bytes 262176 | tf_op jit(solution)/shard_map/ppermute | solution.py:229
  59.1 4.9 %tail_step.1 = (bf16[1024,256]{1,0:T(8,128)(2,1)S(1)}, bf16[512,256]{1,0:T(8,128)(2,1)S(1)}, bf16[512,256]{1,0:T(8,128)(2,1)S(1)}, bf16[512,256]{1,0:T(8,128)(2,1)S(1)}, bf16[512,256]{1,0:T(8,128)(2,1)S(1)}) custom-call(s32[2]{0:T(128)S(1)} %pad_add_fusion.scal, s32[4,1,256]{2,1,0:T(1,128)S(1)} %bitcast.30, bf16[1024,256]{1,0:T(8,128)(2,1)S(1)} %get-tuple-element.17.proj, ...), custom_call_target="tpu_custom_call" | custom-call | flops 3000000000 | bytes 5000000 | tf_op jit(solution)/shard_map/tail_step/pallas_call | solution.py:301
  65.2 2.8 %collective-permute-start.4 = (bf16[512,256]{1,0:T(8,128)(2,1)S(1)}, bf16[512,256]{1,0:T(8,128)(2,1)S(1)}, u32[]{:S(2)}, u32[]{:S(2)}) collective-permute-start(bf16[512,256]{1,0:T(8,128)(2,1)S(1)} %get-tuple-element.21), channel_id=1, source_target_pairs={{2,0},{3,1},{0,2},{1,3},{6,4},{7,5},{4,6},{5,7},{10,8},{11,9},{8,1... | collective-permute-start | bytes 786440 | tf_op jit(solution)/shard_map/ppermute | solution.py:229
  68.4 7.6 %grad_step.1 = (bf16[512,128]{1,0:T(8,128)(2,1)S(1)}, bf16[256,256]{1,0:T(8,128)(2,1)S(1)}, bf16[256,256]{1,0:T(8,128)(2,1)S(1)}, bf16[256,256]{1,0:T(8,128)(2,1)S(1)}, bf16[256,256]{1,0:T(8,128)(2,1)S(1)}) custom-call(s32[2]{0:T(128)S(1)} %pad_add_fusion.scal, s32[1,1024]{1,0:T(1,128)S(1)} %bitcast.32, s32[1,1024]{1,0:T(1,128)S(1)} %bitcast.34, ...), custom_call_target="tpu_custom_call" | custom-call | flops 3000000000 | bytes 6000000 | tf_op jit(solution)/shard_map/grad_step/pallas_call | solution.py:316
  76.0 3.5 %collective-permute-done.4 = bf16[512,256]{1,0:T(8,128)(2,1)S(1)} collective-permute-done((bf16[512,256]{1,0:T(8,128)(2,1)S(1)}, bf16[512,256]{1,0:T(8,128)(2,1)S(1)}, u32[]{:S(2)}, u32[]{:S(2)}) %collective-permute-start.4) | collective-permute-done | bytes 262176 | tf_op jit(solution)/shard_map/ppermute | solution.py:229
  80.4 5.6 %all-to-all-start.2 = ((bf16[64,8,384]{2,1,0:T(8,128)(2,1)}), bf16[64,8,384]{2,1,0:T(8,128)(2,1)S(1)}, u32[]{:S(2)}, u32[]{:S(2)}) async-start(bf16[64,8,384]{2,1,0:T(8,128)(2,1)} %maximum_bitcast_fusion), calls=%async_computation.2 | async-start | bytes 786432 | tf_op jit(solution)/shard_map/all_to_all | solution.py:333
  87.0 2.1 %collective-permute-start.10 = (bf16[256,256]{1,0:T(8,128)(2,1)S(1)}, bf16[256,256]{1,0:T(8,128)(2,1)S(1)}, u32[]{:S(2)}, u32[]{:S(2)}) collective-permute-start(bf16[256,256]{1,0:T(8,128)(2,1)S(1)} %get-tuple-element.30), channel_id=1, source_target_pairs={{2,0},{3,1},{0,2},{1,3},{6,4},{7,5},{4,6},{5,7},{10,8},{11,9},{8,1... | collective-permute-start | bytes 393224 | tf_op jit(solution)/shard_map/ppermute | solution.py:229
  89.8 2.0 %collective-permute-done.9 = bf16[256,256]{1,0:T(8,128)(2,1)S(1)} collective-permute-done((bf16[256,256]{1,0:T(8,128)(2,1)S(1)}, bf16[256,256]{1,0:T(8,128)(2,1)S(1)}, u32[]{:S(2)}, u32[]{:S(2)}) %collective-permute-start.9) | collective-permute-done | bytes 131104 | tf_op jit(solution)/shard_map/ppermute | solution.py:229
  91.8 3.2 %collective-permute-done.10 = bf16[256,256]{1,0:T(8,128)(2,1)S(1)} collective-permute-done((bf16[256,256]{1,0:T(8,128)(2,1)S(1)}, bf16[256,256]{1,0:T(8,128)(2,1)S(1)}, u32[]{:S(2)}, u32[]{:S(2)}) %collective-permute-start.10) | collective-permute-done | bytes 131104 | tf_op jit(solution)/shard_map/ppermute | solution.py:229
  95.1 2.0 %collective-permute-start.14 = (bf16[256,256]{1,0:T(8,128)(2,1)S(1)}, bf16[256,256]{1,0:T(8,128)(2,1)S(1)}, u32[]{:S(2)}, u32[]{:S(2)}) collective-permute-start(bf16[256,256]{1,0:T(8,128)(2,1)S(1)} %add_convert_fusion.1.refs_4_), channel_id=1, source_target_pairs={{3,0},{0,1},{1,2},{2,3},{7,4},{4,5},{5,6},{6,7},{11,8},{8,9},{9,10... | collective-permute-start | bytes 393224 | tf_op jit(solution)/shard_map/ppermute | solution.py:229
  97.1 4.2 %all-to-all-done.2 = bf16[64,8,384]{2,1,0:T(8,128)(2,1)S(1)} async-done(((bf16[64,8,384]{2,1,0:T(8,128)(2,1)}), bf16[64,8,384]{2,1,0:T(8,128)(2,1)S(1)}, u32[]{:S(2)}, u32[]{:S(2)}) %all-to-all-start.2) | async-done | bytes 393248 | tf_op jit(solution)/shard_map/all_to_all | solution.py:333
  102.4 2.1 %collective-permute-start.7 = (bf16[512,256]{1,0:T(8,128)(2,1)S(1)}, bf16[512,256]{1,0:T(8,128)(2,1)S(1)}, u32[]{:S(2)}, u32[]{:S(2)}) collective-permute-start(bf16[512,256]{1,0:T(8,128)(2,1)S(1)} %slice.8.refs_0_), channel_id=1, source_target_pairs={{2,0},{3,1},{0,2},{1,3},{6,4},{7,5},{4,6},{5,7},{10,8},{11,9},{8,1... | collective-permute-start | bytes 786440 | tf_op jit(solution)/shard_map/ppermute | solution.py:229
  105.9 8.5 %all-to-all-start.3 = ((bf16[64,8,128]{2,1,0:T(8,128)(2,1)}), bf16[64,8,128]{2,1,0:T(8,128)(2,1)S(1)}, u32[]{:S(2)}, u32[]{:S(2)}) async-start(bf16[64,8,128]{2,1,0:T(8,128)(2,1)} %broadcast_in_dim.2), calls=%async_computation.3 | async-start | bytes 262144 | tf_op jit(solution)/shard_map/all_to_all | solution.py:338
  114.9 1.7 %collective-permute-start.12 = (bf16[256,256]{1,0:T(8,128)(2,1)S(1)}, bf16[256,256]{1,0:T(8,128)(2,1)S(1)}, u32[]{:S(2)}, u32[]{:S(2)}) collective-permute-start(bf16[256,256]{1,0:T(8,128)(2,1)S(1)} %add_convert_fusion.1.refs_4_), channel_id=1, source_target_pairs={{1,0},{2,1},{3,2},{0,3},{5,4},{6,5},{7,6},{4,7},{9,8},{10,9},{11,1... | collective-permute-start | bytes 393224 | tf_op jit(solution)/shard_map/ppermute | solution.py:229
  117.5 8.0 %all-to-all-done.3 = bf16[64,8,128]{2,1,0:T(8,128)(2,1)S(1)} async-done(((bf16[64,8,128]{2,1,0:T(8,128)(2,1)}), bf16[64,8,128]{2,1,0:T(8,128)(2,1)S(1)}, u32[]{:S(2)}, u32[]{:S(2)}) %all-to-all-start.3) | async-done | bytes 131104 | tf_op jit(solution)/shard_map/all_to_all | solution.py:338
  125.5 1.1 relation_out.1
  126.7 3.5 %owner_add.1 = f32[1024,256]{1,0:T(8,128)} custom-call(s32[2]{0:T(128)S(1)} %pad_add_fusion.scal, s32[4,512]{1,0:T(4,128)S(1)} %list_rows.1.ids, bf16[512,256]{1,0:T(8,128)(2,1)S(1)} %slice.8.refs_0_, bf16[512,256]{1,0:T(8,128)(2,1)S(1)} %collective-permute-done.6.refs_1_, bf16[512,256]{1,0:T(8,128)(2,1)S(1)} %collective-permute-done.7.refs_2_, ...), custom_call_target="tpu_custom_call" | custom-call | flops 1000000000 | bytes 3000000 | tf_op jit(solution)/shard_map/owner_add/pallas_call | solution.py:346
  (43 shorter events, 12.4 us)
Async XLA Ops:
  2.1 22.5 %all-to-all-start = ((s32[64,1,128]{2,1,0:T(1,128)}), s32[64,1,128]{2,1,0:T(1,128)S(1)}, u32[]{:S(2)}, u32[]{:S(2)}) async-start(s32[64,1,128]{2,1,0:T(1,128)} %bitcast.2), calls=%async_computation | async-start | bytes 65536 | tf_op jit(solution)/shard_map/all_to_all | solution.py:249
  24.5 1.0 copy-start
  25.6 23.0 %copy-start.1 = (bf16[1024,256]{1,0:T(8,128)(2,1)S(1)}, bf16[1024,256]{1,0:T(8,128)(2,1)}, u32[]{:S(2)}) copy-start(bf16[1024,256]{1,0:T(8,128)(2,1)} %table.3) | copy-start | bytes 1572868
  25.6 23.0 %copy-start.2 = (bf16[8,8,32,32]{3,2,1,0:T(8,128)(2,1)S(1)}, bf16[8,8,32,32]{3,2,1,0:T(8,128)(2,1)}, u32[]{:S(2)}) copy-start(bf16[8,8,32,32]{3,2,1,0:T(8,128)(2,1)} %param.15) | copy-start | bytes 393220
  43.7 4.8 %copy-start.5 = (s32[1024]{0:T(1024)S(1)}, s32[1024]{0:T(1024)}, u32[]{:S(2)}) copy-start(s32[1024]{0:T(1024)} %param.11) | copy-start | bytes 12292
  43.7 4.8 %copy-start.4 = (s32[1024]{0:T(1024)S(1)}, s32[1024]{0:T(1024)}, u32[]{:S(2)}) copy-start(s32[1024]{0:T(1024)} %param.10) | copy-start | bytes 12292
  43.7 13.4 %collective-permute-start.2 = (bf16[512,256]{1,0:T(8,128)(2,1)S(1)}, bf16[512,256]{1,0:T(8,128)(2,1)S(1)}, u32[]{:S(2)}, u32[]{:S(2)}) collective-permute-start(bf16[512,256]{1,0:T(8,128)(2,1)S(1)} %bitcast.22), channel_id=1, source_target_pairs={{3,0},{0,1},{1,2},{2,3},{7,4},{4,5},{5,6},{6,7},{11,8},{8,9},{9,10... | collective-permute-start | bytes 786440 | tf_op jit(solution)/shard_map/ppermute | solution.py:229
  45.0 14.2 %collective-permute-start.1 = (bf16[512,256]{1,0:T(8,128)(2,1)S(1)}, bf16[512,256]{1,0:T(8,128)(2,1)S(1)}, u32[]{:S(2)}, u32[]{:S(2)}) collective-permute-start(bf16[512,256]{1,0:T(8,128)(2,1)S(1)} %bitcast.23), channel_id=1, source_target_pairs={{2,0},{3,1},{0,2},{1,3},{6,4},{7,5},{4,6},{5,7},{10,8},{11,9},{8,1... | collective-permute-start | bytes 786440 | tf_op jit(solution)/shard_map/ppermute | solution.py:229
  47.4 11.7 %collective-permute-start = (bf16[512,256]{1,0:T(8,128)(2,1)S(1)}, bf16[512,256]{1,0:T(8,128)(2,1)S(1)}, u32[]{:S(2)}, u32[]{:S(2)}) collective-permute-start(bf16[512,256]{1,0:T(8,128)(2,1)S(1)} %bitcast.24), channel_id=1, source_target_pairs={{1,0},{2,1},{3,2},{0,3},{5,4},{6,5},{7,6},{4,7},{9,8},{10,9},{11,1... | collective-permute-start | bytes 786440 | tf_op jit(solution)/shard_map/ppermute | solution.py:229
  57.1 2.1 %copy-start.3 = (s32[1024]{0:T(1024)S(1)}, s32[1024]{0:T(1024)}, u32[]{:S(2)}) copy-start(s32[1024]{0:T(1024)} %param.12) | copy-start | bytes 12292
  64.1 11.9 %collective-permute-start.3 = (bf16[512,256]{1,0:T(8,128)(2,1)S(1)}, bf16[512,256]{1,0:T(8,128)(2,1)S(1)}, u32[]{:S(2)}, u32[]{:S(2)}) collective-permute-start(bf16[512,256]{1,0:T(8,128)(2,1)S(1)} %get-tuple-element.20), channel_id=1, source_target_pairs={{3,0},{0,1},{1,2},{2,3},{7,4},{4,5},{5,6},{6,7},{11,8},{8,9},{9,10... | collective-permute-start | bytes 786440 | tf_op jit(solution)/shard_map/ppermute | solution.py:229
  65.2 14.3 %collective-permute-start.4 = (bf16[512,256]{1,0:T(8,128)(2,1)S(1)}, bf16[512,256]{1,0:T(8,128)(2,1)S(1)}, u32[]{:S(2)}, u32[]{:S(2)}) collective-permute-start(bf16[512,256]{1,0:T(8,128)(2,1)S(1)} %get-tuple-element.21), channel_id=1, source_target_pairs={{2,0},{3,1},{0,2},{1,3},{6,4},{7,5},{4,6},{5,7},{10,8},{11,9},{8,1... | collective-permute-start | bytes 786440 | tf_op jit(solution)/shard_map/ppermute | solution.py:229
  68.0 11.5 %collective-permute-start.5 = (bf16[512,256]{1,0:T(8,128)(2,1)S(1)}, bf16[512,256]{1,0:T(8,128)(2,1)S(1)}, u32[]{:S(2)}, u32[]{:S(2)}) collective-permute-start(bf16[512,256]{1,0:T(8,128)(2,1)S(1)} %get-tuple-element.22), channel_id=1, source_target_pairs={{1,0},{2,1},{3,2},{0,3},{5,4},{6,5},{7,6},{4,7},{9,8},{10,9},{11,1... | collective-permute-start | bytes 786440 | tf_op jit(solution)/shard_map/ppermute | solution.py:229
  80.4 20.9 %all-to-all-start.2 = ((bf16[64,8,384]{2,1,0:T(8,128)(2,1)}), bf16[64,8,384]{2,1,0:T(8,128)(2,1)S(1)}, u32[]{:S(2)}, u32[]{:S(2)}) async-start(bf16[64,8,384]{2,1,0:T(8,128)(2,1)} %maximum_bitcast_fusion), calls=%async_computation.2 | async-start | bytes 786432 | tf_op jit(solution)/shard_map/all_to_all | solution.py:333
  86.0 5.8 %collective-permute-start.9 = (bf16[256,256]{1,0:T(8,128)(2,1)S(1)}, bf16[256,256]{1,0:T(8,128)(2,1)S(1)}, u32[]{:S(2)}, u32[]{:S(2)}) collective-permute-start(bf16[256,256]{1,0:T(8,128)(2,1)S(1)} %get-tuple-element.29), channel_id=1, source_target_pairs={{3,0},{0,1},{1,2},{2,3},{7,4},{4,5},{5,6},{6,7},{11,8},{8,9},{9,10... | collective-permute-start | bytes 393224 | tf_op jit(solution)/shard_map/ppermute | solution.py:229
  87.0 8.0 %collective-permute-start.10 = (bf16[256,256]{1,0:T(8,128)(2,1)S(1)}, bf16[256,256]{1,0:T(8,128)(2,1)S(1)}, u32[]{:S(2)}, u32[]{:S(2)}) collective-permute-start(bf16[256,256]{1,0:T(8,128)(2,1)S(1)} %get-tuple-element.30), channel_id=1, source_target_pairs={{2,0},{3,1},{0,2},{1,3},{6,4},{7,5},{4,6},{5,7},{10,8},{11,9},{8,1... | collective-permute-start | bytes 393224 | tf_op jit(solution)/shard_map/ppermute | solution.py:229
  89.2 5.9 %collective-permute-start.11 = (bf16[256,256]{1,0:T(8,128)(2,1)S(1)}, bf16[256,256]{1,0:T(8,128)(2,1)S(1)}, u32[]{:S(2)}, u32[]{:S(2)}) collective-permute-start(bf16[256,256]{1,0:T(8,128)(2,1)S(1)} %get-tuple-element.31), channel_id=1, source_target_pairs={{1,0},{2,1},{3,2},{0,3},{5,4},{6,5},{7,6},{4,7},{9,8},{10,9},{11,1... | collective-permute-start | bytes 393224 | tf_op jit(solution)/shard_map/ppermute | solution.py:229
  95.1 19.8 %collective-permute-start.14 = (bf16[256,256]{1,0:T(8,128)(2,1)S(1)}, bf16[256,256]{1,0:T(8,128)(2,1)S(1)}, u32[]{:S(2)}, u32[]{:S(2)}) collective-permute-start(bf16[256,256]{1,0:T(8,128)(2,1)S(1)} %add_convert_fusion.1.refs_4_), channel_id=1, source_target_pairs={{3,0},{0,1},{1,2},{2,3},{7,4},{4,5},{5,6},{6,7},{11,8},{8,9},{9,10... | collective-permute-start | bytes 393224 | tf_op jit(solution)/shard_map/ppermute | solution.py:229
  101.4 25.3 %collective-permute-start.8 = (bf16[512,256]{1,0:T(8,128)(2,1)S(1)}, bf16[512,256]{1,0:T(8,128)(2,1)S(1)}, u32[]{:S(2)}, u32[]{:S(2)}) collective-permute-start(bf16[512,256]{1,0:T(8,128)(2,1)S(1)} %slice.8.refs_0_), channel_id=1, source_target_pairs={{3,0},{0,1},{1,2},{2,3},{7,4},{4,5},{5,6},{6,7},{11,8},{8,9},{9,10... | collective-permute-start | bytes 786440 | tf_op jit(solution)/shard_map/ppermute | solution.py:229
  102.4 24.2 %collective-permute-start.7 = (bf16[512,256]{1,0:T(8,128)(2,1)S(1)}, bf16[512,256]{1,0:T(8,128)(2,1)S(1)}, u32[]{:S(2)}, u32[]{:S(2)}) collective-permute-start(bf16[512,256]{1,0:T(8,128)(2,1)S(1)} %slice.8.refs_0_), channel_id=1, source_target_pairs={{2,0},{3,1},{0,2},{1,3},{6,4},{7,5},{4,6},{5,7},{10,8},{11,9},{8,1... | collective-permute-start | bytes 786440 | tf_op jit(solution)/shard_map/ppermute | solution.py:229
  104.5 22.1 %collective-permute-start.6 = (bf16[512,256]{1,0:T(8,128)(2,1)S(1)}, bf16[512,256]{1,0:T(8,128)(2,1)S(1)}, u32[]{:S(2)}, u32[]{:S(2)}) collective-permute-start(bf16[512,256]{1,0:T(8,128)(2,1)S(1)} %slice.8.refs_0_), channel_id=1, source_target_pairs={{1,0},{2,1},{3,2},{0,3},{5,4},{6,5},{7,6},{4,7},{9,8},{10,9},{11,1... | collective-permute-start | bytes 786440 | tf_op jit(solution)/shard_map/ppermute | solution.py:229
  105.9 19.6 %all-to-all-start.3 = ((bf16[64,8,128]{2,1,0:T(8,128)(2,1)}), bf16[64,8,128]{2,1,0:T(8,128)(2,1)S(1)}, u32[]{:S(2)}, u32[]{:S(2)}) async-start(bf16[64,8,128]{2,1,0:T(8,128)(2,1)} %broadcast_in_dim.2), calls=%async_computation.3 | async-start | bytes 262144 | tf_op jit(solution)/shard_map/all_to_all | solution.py:338
  114.4 12.2 %collective-permute-start.13 = (bf16[256,256]{1,0:T(8,128)(2,1)S(1)}, bf16[256,256]{1,0:T(8,128)(2,1)S(1)}, u32[]{:S(2)}, u32[]{:S(2)}) collective-permute-start(bf16[256,256]{1,0:T(8,128)(2,1)S(1)} %add_convert_fusion.1.refs_4_), channel_id=1, source_target_pairs={{2,0},{3,1},{0,2},{1,3},{6,4},{7,5},{4,6},{5,7},{10,8},{11,9},{8,1... | collective-permute-start | bytes 393224 | tf_op jit(solution)/shard_map/ppermute | solution.py:229
  114.9 11.7 %collective-permute-start.12 = (bf16[256,256]{1,0:T(8,128)(2,1)S(1)}, bf16[256,256]{1,0:T(8,128)(2,1)S(1)}, u32[]{:S(2)}, u32[]{:S(2)}) collective-permute-start(bf16[256,256]{1,0:T(8,128)(2,1)S(1)} %add_convert_fusion.1.refs_4_), channel_id=1, source_target_pairs={{1,0},{2,1},{3,2},{0,3},{5,4},{6,5},{7,6},{4,7},{9,8},{10,9},{11,1... | collective-permute-start | bytes 393224 | tf_op jit(solution)/shard_map/ppermute | solution.py:229
  (1 other events, 0.7 us)

commit v2 on v1

--- a/solution.py
+++ b/solution.py
@@ -11,6 +11,7 @@
 BF16 = jnp.bfloat16
 TILE = 256
 SMEM = pl.BlockSpec(memory_space=pltpu.SMEM)
+ANY = pl.BlockSpec(memory_space=pl.ANY)
 CONTRACT_LAST = (((1,), (1,)), ((), ()))
 
 
@@ -54,20 +55,22 @@
     return pl.CostEstimate(flops=int(flops), bytes_accessed=int(nbytes), transcendentals=0)
 
 
-def pick_kernel(share, scal, lists, table, out):
+def pick_kernel(share, scal, lists, table, after, out):
     n = lists.shape[0]
-    wide = jnp.broadcast_to(lists[...].astype(F32)[:, None, :], (n, share, 128))
-    wide = wide.reshape(n * share, 128)
-    shape = (n * share, 128)
+    slots = lists.shape[1]
+    wide = jnp.broadcast_to(lists[...].astype(F32)[:, None, :], (n, share, slots))
+    wide = wide.reshape(n * share, slots)
+    shape = (n * share, slots)
     wanted = iota(shape, 1) == scal[0] * share + iota(shape, 0) % share
     col = jnp.sum(jnp.where(wanted, wide, 0.0), axis=1, keepdims=True).astype(jnp.int32)
     out[...] = dot(hot_rows(col, table.shape[0]), table[...]).astype(BF16)
 
 
-def rows_kernel(share, rels, scal, lists, out):
-    n = lists.shape[0]
+def rows_kernel(share, rels, lists, after, out):
+    n, slots = lists.shape
     wide = n * share
-    ids = jnp.concatenate([lists[...], jnp.zeros((128 - n, 128), jnp.int32)], axis=0)
+    ids = jnp.concatenate([lists[...], jnp.zeros((n, 128 - slots), jnp.int32)], axis=1)
+    ids = jnp.concatenate([ids, jnp.zeros((128 - n, 128), jnp.int32)], axis=0)
     turned = ids.astype(F32).T.astype(jnp.int32)
     spread = jnp.where(iota((128, wide), 1) // share == iota((128, wide), 0), 1.0, 0.0)
     spread = spread.astype(BF16)
@@ -75,10 +78,9 @@
     high = dot((turned >> 5).astype(F32).astype(BF16), spread)
     value = high * 32.0 + low
     slot = iota((128, wide), 0)
-    for c in range(rels):
-        q = (scal[0] + c) % rels
+    for q in range(rels):
         wanted = slot == q * share + iota((128, wide), 1) % share
-        out[c : c + 1, :] = jnp.sum(jnp.where(wanted, value, 0.0), axis=0, keepdims=True).astype(
+        out[q : q + 1, :] = jnp.sum(jnp.where(wanted, value, 0.0), axis=0, keepdims=True).astype(
             jnp.int32
         )
 
@@ -133,7 +135,6 @@
         refs[:n_rel], refs[n_rel : 2 * n_rel + 1], refs[2 * n_rel + 1 :],
     )
     step = pl.program_id(0)
-    edges = pl.num_programs(0) * TILE
     rows = chunks[0].shape[0]
     slots = share * n_rel
     t = tails[0]
@@ -204,16 +205,18 @@
 
 
 def owner_kernel(n_rel, scal, ids, *refs):
-    slots, terms, out = refs[:n_rel], refs[n_rel : 2 * n_rel], refs[2 * n_rel]
+    shares, out = refs[:n_rel], refs[n_rel]
     step = pl.program_id(0)
     rows = out.shape[0]
+    held = ids.shape[1]
     total = jnp.zeros(out.shape, F32)
     for c in range(n_rel):
-        total = total + dot(hot_columns(ids[c : c + 1, :] - step * rows, rows), slots[c][...])
+        row = ids[pl.ds((scal[0] + c) % n_rel, 1), :]
+        total = total + dot(hot_columns(row - step * rows, rows), shares[c][:held, :])
     for c in range(n_rel):
         @pl.when((scal[0] + c) % n_rel == step)
         def _(c=c):
-            out[...] = total + terms[c][...].astype(F32)
+            out[...] = total + shares[c][held:, :].astype(F32)
 
 
 def relation_kernel(r_count, blocks, width, x, out):
@@ -245,8 +248,8 @@
     scal = jnp.concatenate([me.reshape(1), edge_counts])
     shaped = jax.ShapeDtypeStruct
 
-    wide_lists = jnp.pad(request_rows.reshape(parts, slots), ((0, 0), (0, 128 - slots)))
-    lists = lax.all_to_all(wide_lists, "ent", 0, 0, tiled=True)
+    lists = lax.all_to_all(request_rows.reshape(parts, 1, slots), "ent", 0, 0, tiled=True)
+    lists = lists.reshape(parts, slots)
 
     heads = edge_heads.reshape(steps, 1, TILE)
     rels = edge_rels.reshape(steps, 1, TILE)
@@ -278,30 +281,20 @@
 
     picked = pl.pallas_call(
         functools.partial(pick_kernel, share),
-        in_specs=[SMEM, whole((parts, 128)), whole((rows, d))],
+        in_specs=[SMEM, whole((parts, slots)), whole((rows, d)), ANY],
         out_specs=whole((held, d)),
         out_shape=shaped((held, d), BF16),
         compiler_params=params(0),
         cost_estimate=cost(2 * held * rows * d, 1e6),
         name="pick",
-    )(scal, lists, entity_rows)
-    list_rows = pl.pallas_call(
-        functools.partial(rows_kernel, share, n_rel),
-        in_specs=[SMEM, whole((parts, 128))],
-        out_specs=whole((n_rel, held)),
-        out_shape=shaped((n_rel, held), jnp.int32),
-        compiler_params=params(0),
-        cost_estimate=cost(1e8, 1e5),
-        name="list_rows",
-    )(scal, lists)
-
-    fetched = [lax.all_to_all(picked, "ent", 0, 0, tiled=True)]
-    fetched += [ring(fetched[0], n_rel, c) for c in range(1, n_rel)]
+    )(scal, lists, entity_rows, nege)
+    fetched = lax.all_to_all(picked, "ent", 0, 0, tiled=True)
+    fetched = [fetched] + [ring(fetched, n_rel, c) for c in range(1, n_rel)]
 
     grad_proj, *slot_parts = pl.pallas_call(
         functools.partial(tail_kernel, n_rel, share),
         grid=(steps,),
-        in_specs=[SMEM, id_block, edge_block, edge_block] + [whole((held, d))] * n_rel,
+        in_specs=[SMEM, id_block, edge_block, edge_block, ] + [whole((held, d))] * n_rel,
         out_specs=[edge_block] + [whole((held, d))] * n_rel,
         out_shape=[shaped((edges, d), BF16)] + [shaped((held, d), BF16)] * n_rel,
         scratch_shapes=[pltpu.VMEM((edges, d), BF16), pltpu.VMEM((1, edges), jnp.int32)],
@@ -309,6 +302,15 @@
         cost_estimate=cost(3e9, 5e6),
         name="tail_step",
     )(scal, tails, proj, negpart, *fetched)
+    list_rows = pl.pallas_call(
+        functools.partial(rows_kernel, share, n_rel),
+        in_specs=[whole((parts, slots)), ANY],
+        out_specs=whole((n_rel, held)),
+        out_shape=shaped((n_rel, held), jnp.int32),
+        compiler_params=params(0),
+        cost_estimate=cost(1e8, 1e5),
+        name="list_rows",
+    )(lists, grad_proj)
     slot_sum = slot_parts[0].astype(F32)
     for c in range(1, n_rel):
         slot_sum = slot_sum + ring(slot_parts[c], n_rel, n_rel - c).astype(F32)
@@ -331,8 +333,6 @@
 
     packed = jnp.concatenate([slot_sum.astype(BF16), rel_part], axis=1)
     returned = lax.all_to_all(packed, "ent", 0, 0, tiled=True)
-    slot_back = [returned[:, :d]]
-    slot_back += [ring(slot_back[0], n_rel, c) for c in range(1, n_rel)]
     rel_sum = jnp.sum(returned[:, d:].reshape(parts, -1, 128).astype(F32), 0).astype(BF16)
     rel_all = jnp.broadcast_to(rel_sum[None], (parts,) + rel_sum.shape).reshape(-1, 128)
     rel_all = lax.all_to_all(rel_all, "ent", 0, 0, tiled=True)
@@ -340,21 +340,19 @@
     row_sum = row_parts[0].astype(F32)
     for c in range(1, n_rel):
         row_sum = row_sum + ring(row_parts[c], n_rel, n_rel - c).astype(F32)
-    row_terms = [row_sum.astype(BF16)]
-    row_terms += [ring(row_terms[0], n_rel, c) for c in range(1, n_rel)]
+    shares = jnp.concatenate([returned[:, :d], row_sum.astype(BF16)], axis=0)
+    shares = [shares] + [ring(shares, n_rel, c) for c in range(1, n_rel)]
 
     entity_grad = pl.pallas_call(
         functools.partial(owner_kernel, n_rel),
         grid=(n_rel,),
-        in_specs=[SMEM, whole((n_rel, held))]
-        + [whole((held, d))] * n_rel
-        + [whole((rows // n_rel, d))] * n_rel,
+        in_specs=[SMEM, whole((n_rel, held))] + [whole(shares[0].shape)] * n_rel,
         out_specs=pl.BlockSpec((rows // n_rel, d), lambda q: (q, 0)),
         out_shape=shaped((rows, d), F32),
         compiler_params=params(),
         cost_estimate=cost(1e9, 3e6),
         name="owner_add",
-    )(scal, list_rows, *slot_back, *row_terms)
+    )(scal, list_rows, *shares)
     relation_grad = pl.pallas_call(
         functools.partial(relation_kernel, r_count, blocks, width),
         in_specs=[whole(rel_all.shape)],

time: 131 us -> 138 us (1.053)
  starting transfers between devices: 48 us -> 41.7 us
  blocking collectives: 17.1 us -> 23.3 us
  waiting for transfers between devices: 31.6 us -> 36.4 us
  local copies, waits for them, and re-layouts: 3.84 us -> 7.46 us
    ppermute x15 -> x12, waiting for transfers between devices: 10.8 us -> 19.6 us  [ring(): lax.ppermute(x, 'rel', [((k + shift) % n_rel, k) for k in range(n_rel)])]
    all_to_all x1, waiting for transfers between devices: 8.6 us -> 0.01 us  [local(): lax.all_to_all(request_rows.reshape(parts, 1, slots), 'ent', 0, 0, tiled=...]
    all_to_all x1, blocking collectives: 17.1 us -> 23.3 us  [local(): fetched = lax.all_to_all(picked, 'ent', 0, 0, tiled=True)]
    unnamed x15 -> x27, local copies, waits for them, and re-layouts: 2.52 us -> 6.77 us
    ppermute x15 -> x12, starting transfers between devices: 20.8 us -> 16.6 us  [ring(): lax.ppermute(x, 'rel', [((k + shift) % n_rel, k) for k in range(n_rel)])]
    all_to_all x1, waiting for transfers between devices: 7.96 us -> 10.8 us  [local(): rel_all = lax.all_to_all(rel_all, 'ent', 0, 0, tiled=True)]
    all_to_all x1, starting transfers between devices: 8.49 us -> 6.23 us  [local(): rel_all = lax.all_to_all(rel_all, 'ent', 0, 0, tiled=True)]
    all_to_all x1, waiting for transfers between devices: 4.24 us -> 5.99 us  [local(): returned = lax.all_to_all(packed, 'ent', 0, 0, tiled=True)]
  transfers between devices with their start and end apart: 18 -> 15, of which waited for: 7 -> 7; matrix products, arithmetic and copies ran while one was open for 1% -> 1% of each run, Pallas kernels for 13% -> 12%
where the time goes in v2:
time: 138 us
  starting transfers between devices  41.7 us (30%)
  waiting for transfers between devices  36.4 us (26%)
  Pallas kernels  26.3 us (19%)
  blocking collectives  23.3 us (17%)
  local copies, waits for them, and re-layouts  7.46 us (5%)
  between operations  1.44 us (1%)
    all_to_all x1, blocking collectives, local(): fetched = lax.all_to_all(picked, 'ent', 0, 0, tiled=True)  23.3 us
    ppermute x12, waiting for transfers between devices, ring(): lax.ppermute(x, 'rel', [((k + shift) % n_rel, k) for k in range(n_rel)])  19.6 us
    ppermute x12, starting transfers between devices, ring(): lax.ppermute(x, 'rel', [((k + shift) % n_rel, k) for k in range(n_rel)])  16.6 us
    all_to_all x1, starting transfers between devices, local(): lax.all_to_all(request_rows.reshape(parts, 1, slots), 'ent', 0, 0, tiled=...  13.1 us
    all_to_all x1, waiting for transfers between devices, local(): rel_all = lax.all_to_all(rel_all, 'ent', 0, 0, tiled=True)  10.8 us
    pallas_call x1, Pallas kernels, local(): pl.pallas_call(functools.partial(head_kernel, r_count, blocks), grid=(ste...  7.84 us
    pallas_call x1, Pallas kernels, local(): pl.pallas_call(functools.partial(grad_kernel, blocks, n_rel), grid=(r_cou...  7.57 us
    unnamed x27, local copies, waits for them, and re-layouts  6.77 us
  transfers between devices with their start and end apart: 15, of which 7 were waited for; matrix products, arithmetic and copies ran while one was open for 1% of the time, Pallas kernels for 12%

profile of v2, /device:TPU:1, one launch (start us, length us, event | category | flops | bytes accessed | tf_op | source)
XLA Modules:
  0.0 137.8 jit_solution(16813887514874319052)
XLA Ops:
  0.6 1.4 %copy.11 = s32[1,64,32]{2,1,0:T(8,128)} copy(s32[1,64,32]{1,2,0:T(8,128)} %param.9) | data formatting | bytes 16384 | tf_op args[1]
  2.0 13.1 %all-to-all-start = ((s32[64,1,32]{2,1,0:T(1,128)}), s32[64,1,32]{2,1,0:T(1,128)S(1)}, u32[]{:S(2)}, u32[]{:S(2)}) async-start(s32[64,1,32]{2,1,0:T(1,128)} %bitcast.1), calls=%async_computation | async-start | bytes 65536 | tf_op jit(solution)/shard_map/all_to_all | solution.py:251
  18.7 7.8 %head_step.1 = (bf16[1024,256]{1,0:T(8,128)(2,1)S(1)}, f32[1024,256]{1,0:T(8,128)S(1)}, bf16[256,1024]{1,0:T(8,128)(2,1)S(1)}, f32[1024,256]{1,0:T(8,128)S(1)}, bf16[2048,256]{1,0:T(8,128)(2,1)S(1)}) custom-call(s32[2]{0:T(128)S(1)} %pad_add_fusion.scal, s32[4,1,256]{2,1,0:T(1,128)S(1)} %bitcast.30, s32[4,1,256]{2,1,0:T(1,128)S(1)} %bitcast.32, ...), custom_call_target="tpu_custom_call" | custom-call | flops 3000000000 | bytes 6000000 | tf_op jit(solution)/shard_map/head_step/pallas_call | solution.py:261
  30.2 23.3 %all_to_all.36 = bf16[64,8,256]{2,1,0:T(8,128)(2,1)S(1)} all-to-all(bf16[64,8,256]{2,1,0:T(8,128)(2,1)S(1)} %bitcast.20), channel_id=1, replica_groups=mesh['ent'=64,'rel'=4] {'ent'}, dimensions={0} | all-to-all | bytes 524288 | tf_op jit(solution)/shard_map/all_to_all | solution.py:291
  53.5 1.2 collective-permute-start.2
  54.8 2.4 %collective-permute-start.1 = (bf16[512,256]{1,0:T(8,128)(2,1)S(1)}, bf16[512,256]{1,0:T(8,128)(2,1)S(1)}, u32[]{:S(2)}, u32[]{:S(2)}) collective-permute-start(bf16[512,256]{1,0:T(8,128)(2,1)S(1)} %bitcast.25), channel_id=1, source_target_pairs={{2,0},{3,1},{0,2},{1,3},{6,4},{7,5},{4,6},{5,7},{10,8},{11,9},{8,1... | collective-permute-start | bytes 786440 | tf_op jit(solution)/shard_map/ppermute | solution.py:232
  57.2 1.2 collective-permute-start
  58.4 4.0 %collective-permute-done.2.refs_3_ = bf16[512,256]{1,0:T(8,128)(2,1)S(1)} collective-permute-done((bf16[512,256]{1,0:T(8,128)(2,1)S(1)}, bf16[512,256]{1,0:T(8,128)(2,1)S(1)}, u32[]{:S(2)}, u32[]{:S(2)}) %collective-permute-start.2) | collective-permute-done | bytes 262176 | tf_op jit(solution)/shard_map/ppermute | solution.py:232
  62.3 6.6 %collective-permute-done.1.refs_2_ = bf16[512,256]{1,0:T(8,128)(2,1)S(1)} collective-permute-done((bf16[512,256]{1,0:T(8,128)(2,1)S(1)}, bf16[512,256]{1,0:T(8,128)(2,1)S(1)}, u32[]{:S(2)}, u32[]{:S(2)}) %collective-permute-start.1) | collective-permute-done | bytes 262176 | tf_op jit(solution)/shard_map/ppermute | solution.py:232
  69.0 4.9 %tail_step.1 = (bf16[1024,256]{1,0:T(8,128)(2,1)S(1)}, bf16[512,256]{1,0:T(8,128)(2,1)S(1)}, bf16[512,256]{1,0:T(8,128)(2,1)S(1)}, bf16[512,256]{1,0:T(8,128)(2,1)S(1)}, bf16[512,256]{1,0:T(8,128)(2,1)S(1)}) custom-call(s32[2]{0:T(128)S(1)} %pad_add_fusion.scal, s32[4,1,256]{2,1,0:T(1,128)S(1)} %bitcast.29, bf16[1024,256]{1,0:T(8,128)(2,1)S(1)} %copy-done.12, ...), custom_call_target="tpu_custom_call" | custom-call | flops 3000000000 | bytes 5000000 | tf_op jit(solution)/shard_map/tail_step/pallas_call | solution.py:294
  73.9 1.1 collective-permute-start.3
  75.0 2.8 %collective-permute-start.4 = (bf16[512,256]{1,0:T(8,128)(2,1)S(1)}, bf16[512,256]{1,0:T(8,128)(2,1)S(1)}, u32[]{:S(2)}, u32[]{:S(2)}) collective-permute-start(bf16[512,256]{1,0:T(8,128)(2,1)S(1)} %get-tuple-element.23), channel_id=1, source_target_pairs={{2,0},{3,1},{0,2},{1,3},{6,4},{7,5},{4,6},{5,7},{10,8},{11,9},{8,1... | collective-permute-start | bytes 786440 | tf_op jit(solution)/shard_map/ppermute | solution.py:232
  78.2 7.6 %grad_step.1 = (bf16[512,128]{1,0:T(8,128)(2,1)S(1)}, bf16[256,256]{1,0:T(8,128)(2,1)S(1)}, bf16[256,256]{1,0:T(8,128)(2,1)S(1)}, bf16[256,256]{1,0:T(8,128)(2,1)S(1)}, bf16[256,256]{1,0:T(8,128)(2,1)S(1)}) custom-call(s32[2]{0:T(128)S(1)} %pad_add_fusion.scal, s32[1,1024]{1,0:T(1,128)S(1)} %bitcast.31, s32[1,1024]{1,0:T(1,128)S(1)} %bitcast.33, ...), custom_call_target="tpu_custom_call" | custom-call | flops 3000000000 | bytes 6000000 | tf_op jit(solution)/shard_map/grad_step/pallas_call | solution.py:318
  85.8 3.5 %collective-permute-done.4 = bf16[512,256]{1,0:T(8,128)(2,1)S(1)} collective-permute-done((bf16[512,256]{1,0:T(8,128)(2,1)S(1)}, bf16[512,256]{1,0:T(8,128)(2,1)S(1)}, u32[]{:S(2)}, u32[]{:S(2)}) %collective-permute-start.4) | collective-permute-done | bytes 262176 | tf_op jit(solution)/shard_map/ppermute | solution.py:232
  90.3 5.8 %all-to-all-start.2 = ((bf16[64,8,384]{2,1,0:T(8,128)(2,1)}), bf16[64,8,384]{2,1,0:T(8,128)(2,1)S(1)}, u32[]{:S(2)}, u32[]{:S(2)}) async-start(bf16[64,8,384]{2,1,0:T(8,128)(2,1)} %maximum_bitcast_fusion), calls=%async_computation.2 | async-start | bytes 786432 | tf_op jit(solution)/shard_map/all_to_all | solution.py:335
  97.0 2.2 %collective-permute-start.7 = (bf16[256,256]{1,0:T(8,128)(2,1)S(1)}, bf16[256,256]{1,0:T(8,128)(2,1)S(1)}, u32[]{:S(2)}, u32[]{:S(2)}) collective-permute-start(bf16[256,256]{1,0:T(8,128)(2,1)S(1)} %get-tuple-element.30), channel_id=1, source_target_pairs={{2,0},{3,1},{0,2},{1,3},{6,4},{7,5},{4,6},{5,7},{10,8},{11,9},{8,1... | collective-permute-start | bytes 393224 | tf_op jit(solution)/shard_map/ppermute | solution.py:232
  99.7 2.2 %collective-permute-done.6 = bf16[256,256]{1,0:T(8,128)(2,1)S(1)} collective-permute-done((bf16[256,256]{1,0:T(8,128)(2,1)S(1)}, bf16[256,256]{1,0:T(8,128)(2,1)S(1)}, u32[]{:S(2)}, u32[]{:S(2)}) %collective-permute-start.6) | collective-permute-done | bytes 131104 | tf_op jit(solution)/shard_map/ppermute | solution.py:232
  101.9 3.2 %collective-permute-done.7 = bf16[256,256]{1,0:T(8,128)(2,1)S(1)} collective-permute-done((bf16[256,256]{1,0:T(8,128)(2,1)S(1)}, bf16[256,256]{1,0:T(8,128)(2,1)S(1)}, u32[]{:S(2)}, u32[]{:S(2)}) %collective-permute-start.7) | collective-permute-done | bytes 131104 | tf_op jit(solution)/shard_map/ppermute | solution.py:232
  105.2 6.0 %all-to-all-done.2 = bf16[64,8,384]{2,1,0:T(8,128)(2,1)S(1)} async-done(((bf16[64,8,384]{2,1,0:T(8,128)(2,1)}), bf16[64,8,384]{2,1,0:T(8,128)(2,1)S(1)}, u32[]{:S(2)}, u32[]{:S(2)}) %all-to-all-start.2) | async-done | bytes 393248 | tf_op jit(solution)/shard_map/all_to_all | solution.py:335
  112.2 2.2 %collective-permute-start.10 = (bf16[768,256]{1,0:T(8,128)(2,1)S(1)}, bf16[768,256]{1,0:T(8,128)(2,1)S(1)}, u32[]{:S(2)}, u32[]{:S(2)}) collective-permute-start(bf16[768,256]{1,0:T(8,128)(2,1)S(1)} %pad_maximum_fusion.refs_0_), channel_id=1, source_target_pairs={{2,0},{3,1},{0,2},{1,3},{6,4},{7,5},{4,6},{5,7},{10,8},{11,9},{8,1... | collective-permute-start | bytes 1179656 | tf_op jit(solution)/shard_map/ppermute | solution.py:232
  115.8 6.2 %all-to-all-start.3 = ((bf16[64,8,128]{2,1,0:T(8,128)(2,1)}), bf16[64,8,128]{2,1,0:T(8,128)(2,1)S(1)}, u32[]{:S(2)}, u32[]{:S(2)}) async-start(bf16[64,8,128]{2,1,0:T(8,128)(2,1)} %broadcast_in_dim.2), calls=%async_computation.3 | async-start | bytes 262144 | tf_op jit(solution)/shard_map/all_to_all | solution.py:338
  122.3 10.8 %all-to-all-done.3 = bf16[64,8,128]{2,1,0:T(8,128)(2,1)S(1)} async-done(((bf16[64,8,128]{2,1,0:T(8,128)(2,1)}), bf16[64,8,128]{2,1,0:T(8,128)(2,1)S(1)}, u32[]{:S(2)}, u32[]{:S(2)}) %all-to-all-start.3) | async-done | bytes 131104 | tf_op jit(solution)/shard_map/all_to_all | solution.py:338
  133.1 1.1 relation_out.1
  134.3 3.5 %owner_add.1 = f32[1024,256]{1,0:T(8,128)} custom-call(s32[2]{0:T(128)S(1)} %pad_add_fusion.scal, s32[4,512]{1,0:T(4,128)S(1)} %list_rows.1.ids, bf16[768,256]{1,0:T(8,128)(2,1)S(1)} %pad_maximum_fusion.refs_0_, bf16[768,256]{1,0:T(8,128)(2,1)S(1)} %collective-permute-done.9.refs_1_, bf16[768,256]{1,0:T(8,128)(2,1)S(1)} %collective-permute-done.10.refs_2_, ...), custom_call_target="tpu_custom_call" | custom-call | flops 1000000000 | bytes 3000000 | tf_op jit(solution)/shard_map/owner_add/pallas_call | solution.py:346
  (49 shorter events, 12.1 us)
Async XLA Ops:
  2.0 27.1 %all-to-all-start = ((s32[64,1,32]{2,1,0:T(1,128)}), s32[64,1,32]{2,1,0:T(1,128)S(1)}, u32[]{:S(2)}, u32[]{:S(2)}) async-start(s32[64,1,32]{2,1,0:T(1,128)} %bitcast.1), calls=%async_computation | async-start | bytes 65536 | tf_op jit(solution)/shard_map/all_to_all | solution.py:251
  16.6 1.0 copy-start
  17.7 1.0 copy-start.2
  18.7 10.4 %copy-start.1 = (bf16[1024,256]{1,0:T(8,128)(2,1)S(1)}, bf16[1024,256]{1,0:T(8,128)(2,1)}, u32[]{:S(2)}) copy-start(bf16[1024,256]{1,0:T(8,128)(2,1)} %table.3) | copy-start | bytes 1572868
  26.5 1.0 copy-start.7
  27.5 0.8 copy-start.9
  29.1 39.8 %copy-start.8 = (f32[1024,256]{1,0:T(8,128)S(1)}, f32[1024,256]{1,0:T(8,128)}, u32[]{:S(2)}) copy-start(f32[1024,256]{1,0:T(8,128)} %copy-done.7) | copy-start | bytes 3145732
  30.2 38.7 %copy-start.12 = (bf16[1024,256]{1,0:T(8,128)(2,1)S(1)}, bf16[1024,256]{1,0:T(8,128)(2,1)}, u32[]{:S(2)}) copy-start(bf16[1024,256]{1,0:T(8,128)(2,1)} %copy-done.11) | copy-start | bytes 1572868
  53.5 15.4 %copy-start.3 = (s32[1024]{0:T(1024)S(1)}, s32[1024]{0:T(1024)}, u32[]{:S(2)}) copy-start(s32[1024]{0:T(1024)} %param.12) | copy-start | bytes 12292
  53.5 8.8 %collective-permute-start.2 = (bf16[512,256]{1,0:T(8,128)(2,1)S(1)}, bf16[512,256]{1,0:T(8,128)(2,1)S(1)}, u32[]{:S(2)}, u32[]{:S(2)}) collective-permute-start(bf16[512,256]{1,0:T(8,128)(2,1)S(1)} %bitcast.24), channel_id=1, source_target_pairs={{3,0},{0,1},{1,2},{2,3},{7,4},{4,5},{5,6},{6,7},{11,8},{8,9},{9,10... | collective-permute-start | bytes 786440 | tf_op jit(solution)/shard_map/ppermute | solution.py:232
  54.8 14.2 %collective-permute-start.1 = (bf16[512,256]{1,0:T(8,128)(2,1)S(1)}, bf16[512,256]{1,0:T(8,128)(2,1)S(1)}, u32[]{:S(2)}, u32[]{:S(2)}) collective-permute-start(bf16[512,256]{1,0:T(8,128)(2,1)S(1)} %bitcast.25), channel_id=1, source_target_pairs={{2,0},{3,1},{0,2},{1,3},{6,4},{7,5},{4,6},{5,7},{10,8},{11,9},{8,1... | collective-permute-start | bytes 786440 | tf_op jit(solution)/shard_map/ppermute | solution.py:232
  57.2 11.8 %collective-permute-start = (bf16[512,256]{1,0:T(8,128)(2,1)S(1)}, bf16[512,256]{1,0:T(8,128)(2,1)S(1)}, u32[]{:S(2)}, u32[]{:S(2)}) collective-permute-start(bf16[512,256]{1,0:T(8,128)(2,1)S(1)} %bitcast.26), channel_id=1, source_target_pairs={{1,0},{2,1},{3,2},{0,3},{5,4},{6,5},{7,6},{4,7},{9,8},{10,9},{11,1... | collective-permute-start | bytes 786440 | tf_op jit(solution)/shard_map/ppermute | solution.py:232
  69.0 9.3 %copy-start.10 = (bf16[256,1024]{1,0:T(8,128)(2,1)S(1)}, bf16[256,1024]{1,0:T(8,128)(2,1)}, u32[]{:S(2)}) copy-start(bf16[256,1024]{1,0:T(8,128)(2,1)} %copy-done.9) | copy-start | bytes 1572868
  73.9 11.9 %collective-permute-start.3 = (bf16[512,256]{1,0:T(8,128)(2,1)S(1)}, bf16[512,256]{1,0:T(8,128)(2,1)S(1)}, u32[]{:S(2)}, u32[]{:S(2)}) collective-permute-start(bf16[512,256]{1,0:T(8,128)(2,1)S(1)} %get-tuple-element.22), channel_id=1, source_target_pairs={{3,0},{0,1},{1,2},{2,3},{7,4},{4,5},{5,6},{6,7},{11,8},{8,9},{9,10... | collective-permute-start | bytes 786440 | tf_op jit(solution)/shard_map/ppermute | solution.py:232
  75.0 14.3 %collective-permute-start.4 = (bf16[512,256]{1,0:T(8,128)(2,1)S(1)}, bf16[512,256]{1,0:T(8,128)(2,1)S(1)}, u32[]{:S(2)}, u32[]{:S(2)}) collective-permute-start(bf16[512,256]{1,0:T(8,128)(2,1)S(1)} %get-tuple-element.23), channel_id=1, source_target_pairs={{2,0},{3,1},{0,2},{1,3},{6,4},{7,5},{4,6},{5,7},{10,8},{11,9},{8,1... | collective-permute-start | bytes 786440 | tf_op jit(solution)/shard_map/ppermute | solution.py:232
  77.8 11.5 %collective-permute-start.5 = (bf16[512,256]{1,0:T(8,128)(2,1)S(1)}, bf16[512,256]{1,0:T(8,128)(2,1)S(1)}, u32[]{:S(2)}, u32[]{:S(2)}) collective-permute-start(bf16[512,256]{1,0:T(8,128)(2,1)S(1)} %get-tuple-element.24), channel_id=1, source_target_pairs={{1,0},{2,1},{3,2},{0,3},{5,4},{6,5},{7,6},{4,7},{9,8},{10,9},{11,1... | collective-permute-start | bytes 786440 | tf_op jit(solution)/shard_map/ppermute | solution.py:232
  90.3 20.9 %all-to-all-start.2 = ((bf16[64,8,384]{2,1,0:T(8,128)(2,1)}), bf16[64,8,384]{2,1,0:T(8,128)(2,1)S(1)}, u32[]{:S(2)}, u32[]{:S(2)}) async-start(bf16[64,8,384]{2,1,0:T(8,128)(2,1)} %maximum_bitcast_fusion), calls=%async_computation.2 | async-start | bytes 786432 | tf_op jit(solution)/shard_map/all_to_all | solution.py:335
  96.0 5.9 %collective-permute-start.6 = (bf16[256,256]{1,0:T(8,128)(2,1)S(1)}, bf16[256,256]{1,0:T(8,128)(2,1)S(1)}, u32[]{:S(2)}, u32[]{:S(2)}) collective-permute-start(bf16[256,256]{1,0:T(8,128)(2,1)S(1)} %get-tuple-element.29), channel_id=1, source_target_pairs={{3,0},{0,1},{1,2},{2,3},{7,4},{4,5},{5,6},{6,7},{11,8},{8,9},{9,10... | collective-permute-start | bytes 393224 | tf_op jit(solution)/shard_map/ppermute | solution.py:232
  97.0 8.1 %collective-permute-start.7 = (bf16[256,256]{1,0:T(8,128)(2,1)S(1)}, bf16[256,256]{1,0:T(8,128)(2,1)S(1)}, u32[]{:S(2)}, u32[]{:S(2)}) collective-permute-start(bf16[256,256]{1,0:T(8,128)(2,1)S(1)} %get-tuple-element.30), channel_id=1, source_target_pairs={{2,0},{3,1},{0,2},{1,3},{6,4},{7,5},{4,6},{5,7},{10,8},{11,9},{8,1... | collective-permute-start | bytes 393224 | tf_op jit(solution)/shard_map/ppermute | solution.py:232
  99.2 5.9 %collective-permute-start.8 = (bf16[256,256]{1,0:T(8,128)(2,1)S(1)}, bf16[256,256]{1,0:T(8,128)(2,1)S(1)}, u32[]{:S(2)}, u32[]{:S(2)}) collective-permute-start(bf16[256,256]{1,0:T(8,128)(2,1)S(1)} %get-tuple-element.31), channel_id=1, source_target_pairs={{1,0},{2,1},{3,2},{0,3},{5,4},{6,5},{7,6},{4,7},{9,8},{10,9},{11,1... | collective-permute-start | bytes 393224 | tf_op jit(solution)/shard_map/ppermute | solution.py:232
  111.3 23.0 %collective-permute-start.11 = (bf16[768,256]{1,0:T(8,128)(2,1)S(1)}, bf16[768,256]{1,0:T(8,128)(2,1)S(1)}, u32[]{:S(2)}, u32[]{:S(2)}) collective-permute-start(bf16[768,256]{1,0:T(8,128)(2,1)S(1)} %pad_maximum_fusion.refs_0_), channel_id=1, source_target_pairs={{3,0},{0,1},{1,2},{2,3},{7,4},{4,5},{5,6},{6,7},{11,8},{8,9},{9,10... | collective-permute-start | bytes 1179656 | tf_op jit(solution)/shard_map/ppermute | solution.py:232
  112.2 22.0 %collective-permute-start.10 = (bf16[768,256]{1,0:T(8,128)(2,1)S(1)}, bf16[768,256]{1,0:T(8,128)(2,1)S(1)}, u32[]{:S(2)}, u32[]{:S(2)}) collective-permute-start(bf16[768,256]{1,0:T(8,128)(2,1)S(1)} %pad_maximum_fusion.refs_0_), channel_id=1, source_target_pairs={{2,0},{3,1},{0,2},{1,3},{6,4},{7,5},{4,6},{5,7},{10,8},{11,9},{8,1... | collective-permute-start | bytes 1179656 | tf_op jit(solution)/shard_map/ppermute | solution.py:232
  114.4 19.9 %collective-permute-start.9 = (bf16[768,256]{1,0:T(8,128)(2,1)S(1)}, bf16[768,256]{1,0:T(8,128)(2,1)S(1)}, u32[]{:S(2)}, u32[]{:S(2)}) collective-permute-start(bf16[768,256]{1,0:T(8,128)(2,1)S(1)} %pad_maximum_fusion.refs_0_), channel_id=1, source_target_pairs={{1,0},{2,1},{3,2},{0,3},{5,4},{6,5},{7,6},{4,7},{9,8},{10,9},{11,1... | collective-permute-start | bytes 1179656 | tf_op jit(solution)/shard_map/ppermute | solution.py:232
  115.8 17.3 %all-to-all-start.3 = ((bf16[64,8,128]{2,1,0:T(8,128)(2,1)}), bf16[64,8,128]{2,1,0:T(8,128)(2,1)S(1)}, u32[]{:S(2)}, u32[]{:S(2)}) async-start(bf16[64,8,128]{2,1,0:T(8,128)(2,1)} %broadcast_in_dim.2), calls=%async_computation.3 | async-start | bytes 262144 | tf_op jit(solution)/shard_map/all_to_all | solution.py:338
  (4 other events, 2.9 us)

commit v3 on v2

--- a/solution.py
+++ b/solution.py
@@ -47,7 +47,7 @@
 def params(steps=1):
     return pltpu.CompilerParams(
         dimension_semantics=("arbitrary",) * (1 if steps else 0),
-        vmem_limit_bytes=48 * 1024 * 1024,
+        vmem_limit_bytes=(24 if steps else 12) * 1024 * 1024,
     )
 
 
@@ -55,7 +55,11 @@
     return pl.CostEstimate(flops=int(flops), bytes_accessed=int(nbytes), transcendentals=0)
 
 
-def pick_kernel(share, scal, lists, table, after, out):
+def stage_kernel(table, out):
+    out[...] = table[...]
+
+
+def pick_kernel(share, scal, lists, table, out):
     n = lists.shape[0]
     slots = lists.shape[1]
     wide = jnp.broadcast_to(lists[...].astype(F32)[:, None, :], (n, share, slots))
@@ -66,7 +70,7 @@
     out[...] = dot(hot_rows(col, table.shape[0]), table[...]).astype(BF16)
 
 
-def rows_kernel(share, rels, lists, after, out):
+def rows_kernel(share, scal, lists, after, out):
     n, slots = lists.shape
     wide = n * share
     ids = jnp.concatenate([lists[...], jnp.zeros((n, 128 - slots), jnp.int32)], axis=1)
@@ -76,13 +80,9 @@
     spread = spread.astype(BF16)
     low = dot((turned & 31).astype(F32).astype(BF16), spread)
     high = dot((turned >> 5).astype(F32).astype(BF16), spread)
-    value = high * 32.0 + low
-    slot = iota((128, wide), 0)
-    for q in range(rels):
-        wanted = slot == q * share + iota((128, wide), 1) % share
-        out[q : q + 1, :] = jnp.sum(jnp.where(wanted, value, 0.0), axis=0, keepdims=True).astype(
-            jnp.int32
-        )
+    wanted = iota((128, wide), 0) == scal[0] * share + iota((128, wide), 1) % share
+    value = jnp.where(wanted, high * 32.0 + low, 0.0)
+    out[...] = jnp.sum(value, axis=0, keepdims=True).astype(jnp.int32)
 
 
 def head_kernel(
@@ -162,10 +162,9 @@
 
 
 def grad_kernel(
-    blocks, n_rel, scal, heads, rels, gp, turned, nege, bd,
-    rel_out, *refs,
+    blocks, heads, rels, gp, turned, nege, bd,
+    rel_out, rows_out, head_acc,
 ):
-    outs, (head_acc, rows_acc) = refs[:n_rel], refs[n_rel:]
     step = pl.program_id(0)
     edges, d = gp.shape
     width = d // blocks
@@ -194,29 +193,28 @@
 
     @pl.when(step == pl.num_programs(0) - 1)
     def _():
-        rows = nege.shape[0] // n_rel
         head_grad = head_acc[...].astype(BF16)
         for k in range(nege.shape[0] // TILE):
             part = slice(k * TILE, (k + 1) * TILE)
-            rows_acc[part, :] = nege[part, :] + dot(hot_columns(heads[...] - k * TILE, TILE), head_grad)
-        for c in range(n_rel):
-            start = pl.multiple_of((scal[0] + c) % n_rel * rows, rows)
-            outs[c][...] = rows_acc[pl.ds(start, rows), :].astype(BF16)
-
-
-def owner_kernel(n_rel, scal, ids, *refs):
-    shares, out = refs[:n_rel], refs[n_rel]
-    step = pl.program_id(0)
-    rows = out.shape[0]
-    held = ids.shape[1]
-    total = jnp.zeros(out.shape, F32)
+            rows_out[part, :] = nege[part, :] + dot(hot_columns(heads[...] - k * TILE, TILE), head_grad)
+
+
+def owner_kernel(n_rel, scal, ids, returned, terms, *outs):
+    d = terms.shape[1]
+    rows = terms.shape[0] // n_rel
     for c in range(n_rel):
-        row = ids[pl.ds((scal[0] + c) % n_rel, 1), :]
-        total = total + dot(hot_columns(row - step * rows, rows), shares[c][:held, :])
+        start = pl.multiple_of((scal[0] + c) % n_rel * rows, rows)
+        total = terms[pl.ds(start, rows), :]
+        total = total + dot(hot_columns(ids[...] - start, rows), returned[:, :d])
+        outs[c][...] = total.astype(BF16)
+
+
+def place_kernel(n_rel, scal, *refs):
+    out = refs[n_rel]
+    rows = out.shape[0] // n_rel
     for c in range(n_rel):
-        @pl.when((scal[0] + c) % n_rel == step)
-        def _(c=c):
-            out[...] = total + shares[c][held:, :].astype(F32)
+        start = pl.multiple_of((scal[0] + c) % n_rel * rows, rows)
+        out[pl.ds(start, rows), :] = refs[c][...].astype(F32)
 
 
 def relation_kernel(r_count, blocks, width, x, out):
@@ -258,6 +256,24 @@
     id_block = pl.BlockSpec((1, 1, TILE), lambda i: (i, 0, 0))
     edge_block = pl.BlockSpec((TILE, d), lambda i: (i, 0))
 
+    table = pl.pallas_call(
+        stage_kernel,
+        in_specs=[whole((rows, d))],
+        out_specs=whole((rows, d)),
+        out_shape=shaped((rows, d), BF16),
+        compiler_params=params(0),
+        cost_estimate=cost(1e6, 1e6),
+        name="stage",
+    )(entity_rows)
+    picked = pl.pallas_call(
+        functools.partial(pick_kernel, share),
+        in_specs=[SMEM, whole((parts, slots)), whole((rows, d))],
+        out_specs=whole((held, d)),
+        out_shape=shaped((held, d), BF16),
+        compiler_params=params(0),
+        cost_estimate=cost(2 * held * rows * d, 1e6),
+        name="pick",
+    )(scal, lists, table)
     proj, negpart, turned, nege, bd = pl.pallas_call(
         functools.partial(head_kernel, r_count, blocks),
         grid=(steps,),
@@ -279,15 +295,6 @@
         name="head_step",
     )(scal, heads, rels, negs, entity_rows, relation_blocks.reshape(r_count * d, width))
 
-    picked = pl.pallas_call(
-        functools.partial(pick_kernel, share),
-        in_specs=[SMEM, whole((parts, slots)), whole((rows, d)), ANY],
-        out_specs=whole((held, d)),
-        out_shape=shaped((held, d), BF16),
-        compiler_params=params(0),
-        cost_estimate=cost(2 * held * rows * d, 1e6),
-        name="pick",
-    )(scal, lists, entity_rows, nege)
     fetched = lax.all_to_all(picked, "ent", 0, 0, tiled=True)
     fetched = [fetched] + [ring(fetched, n_rel, c) for c in range(1, n_rel)]
 
@@ -303,33 +310,32 @@
         name="tail_step",
     )(scal, tails, proj, negpart, *fetched)
     list_rows = pl.pallas_call(
-        functools.partial(rows_kernel, share, n_rel),
-        in_specs=[whole((parts, slots)), ANY],
-        out_specs=whole((n_rel, held)),
-        out_shape=shaped((n_rel, held), jnp.int32),
+        functools.partial(rows_kernel, share),
+        in_specs=[SMEM, whole((parts, slots)), ANY],
+        out_specs=whole((1, held)),
+        out_shape=shaped((1, held), jnp.int32),
         compiler_params=params(0),
         cost_estimate=cost(1e8, 1e5),
         name="list_rows",
-    )(lists, grad_proj)
+    )(scal, lists, grad_proj)
     slot_sum = slot_parts[0].astype(F32)
     for c in range(1, n_rel):
         slot_sum = slot_sum + ring(slot_parts[c], n_rel, n_rel - c).astype(F32)
 
-    rel_part, *row_parts = pl.pallas_call(
-        functools.partial(grad_kernel, blocks, n_rel),
+    rel_part, row_terms = pl.pallas_call(
+        functools.partial(grad_kernel, blocks),
         grid=(r_count,),
         in_specs=[
-            SMEM, whole((1, edges)), whole((1, edges)), whole((edges, d)), whole((d, edges)),
+            whole((1, edges)), whole((1, edges)), whole((edges, d)), whole((d, edges)),
             whole((rows, d)), pl.BlockSpec((d, d), lambda r: (r, 0)),
         ],
-        out_specs=[whole((r_count * width * d // 128, 128))] + [whole((rows // n_rel, d))] * n_rel,
-        out_shape=[shaped((r_count * width * d // 128, 128), BF16)]
-        + [shaped((rows // n_rel, d), BF16)] * n_rel,
-        scratch_shapes=[pltpu.VMEM((edges, d), F32), pltpu.VMEM((rows, d), F32)],
+        out_specs=[whole((r_count * width * d // 128, 128)), whole((rows, d))],
+        out_shape=[shaped((r_count * width * d // 128, 128), BF16), shaped((rows, d), F32)],
+        scratch_shapes=[pltpu.VMEM((edges, d), F32)],
         compiler_params=params(),
         cost_estimate=cost(3e9, 6e6),
         name="grad_step",
-    )(scal, edge_heads.reshape(1, edges), edge_rels.reshape(1, edges), grad_proj, turned, nege, bd)
+    )(edge_heads.reshape(1, edges), edge_rels.reshape(1, edges), grad_proj, turned, nege, bd)
 
     packed = jnp.concatenate([slot_sum.astype(BF16), rel_part], axis=1)
     returned = lax.all_to_all(packed, "ent", 0, 0, tiled=True)
@@ -337,22 +343,30 @@
     rel_all = jnp.broadcast_to(rel_sum[None], (parts,) + rel_sum.shape).reshape(-1, 128)
     rel_all = lax.all_to_all(rel_all, "ent", 0, 0, tiled=True)
 
+    row_parts = pl.pallas_call(
+        functools.partial(owner_kernel, n_rel),
+        in_specs=[SMEM, whole((1, held)), whole(returned.shape), whole((rows, d))],
+        out_specs=[whole((rows // n_rel, d))] * n_rel,
+        out_shape=[shaped((rows // n_rel, d), BF16)] * n_rel,
+        compiler_params=params(0),
+        cost_estimate=cost(3e8, 2e6),
+        name="owner_add",
+    )(scal, list_rows, returned, row_terms)
     row_sum = row_parts[0].astype(F32)
     for c in range(1, n_rel):
         row_sum = row_sum + ring(row_parts[c], n_rel, n_rel - c).astype(F32)
-    shares = jnp.concatenate([returned[:, :d], row_sum.astype(BF16)], axis=0)
-    shares = [shares] + [ring(shares, n_rel, c) for c in range(1, n_rel)]
-
+    row_sum = row_sum.astype(BF16)
+    row_sums = [row_sum] + [ring(row_sum, n_rel, c) for c in range(1, n_rel)]
     entity_grad = pl.pallas_call(
-        functools.partial(owner_kernel, n_rel),
-        grid=(n_rel,),
-        in_specs=[SMEM, whole((n_rel, held))] + [whole(shares[0].shape)] * n_rel,
-        out_specs=pl.BlockSpec((rows // n_rel, d), lambda q: (q, 0)),
+        functools.partial(place_kernel, n_rel),
+        in_specs=[SMEM] + [whole((rows // n_rel, d))] * n_rel,
+        out_specs=whole((rows, d)),
         out_shape=shaped((rows, d), F32),
-        compiler_params=params(),
-        cost_estimate=cost(1e9, 3e6),
-        name="owner_add",
-    )(scal, list_rows, *shares)
+        compiler_params=params(0),
+        cost_estimate=cost(1e6, 1.5e6),
+        name="place_rows",
+    )(scal, *row_sums)
+    rel_all, entity_grad = lax.optimization_barrier((rel_all, entity_grad))
     relation_grad = pl.pallas_call(
         functools.partial(relation_kernel, r_count, blocks, width),
         in_specs=[whole(rel_all.shape)],

time: 138 us -> 125 us (0.906)
  blocking collectives: 23.3 us -> 17.1 us
  local copies, waits for them, and re-layouts: 7.46 us -> 3.81 us
  waiting for transfers between devices: 36.4 us -> 34.1 us
    all_to_all x1, waiting for transfers between devices: 10.8 us -> 0.37 us  [local(): rel_all = lax.all_to_all(rel_all, 'ent', 0, 0, tiled=True)]
    all_to_all x1, waiting for transfers between devices: 5.99 us -> 14.5 us  [local(): returned = lax.all_to_all(packed, 'ent', 0, 0, tiled=True)]
    ppermute x12, waiting for transfers between devices: 19.6 us -> 11.7 us  [ring(): lax.ppermute(x, 'rel', [((k + shift) % n_rel, k) for k in range(n_rel)])]
    all_to_all x1, waiting for transfers between devices: 0.01 us -> 7.52 us  [local(): lax.all_to_all(request_rows.reshape(parts, 1, slots), 'ent', 0, 0, tiled=...]
    all_to_all x1, blocking collectives: 23.3 us -> 17.1 us  [local(): fetched = lax.all_to_all(picked, 'ent', 0, 0, tiled=True)]
    unnamed x27 -> x15, local copies, waits for them, and re-layouts: 6.77 us -> 3.14 us
    pallas_call x3 -> x5, Pallas kernels: 11.3 us -> 10.4 us  [the longest x1 6.92 us: local(): pl.pallas_call(functools.partial(grad_kernel, blocks), grid=(r_count,), i...]
  transfers between devices with their start and end apart: 15 -> 15, of which waited for: 7 -> 8; matrix products, arithmetic and copies ran while one was open for 1% -> 1% of each run, Pallas kernels for 12% -> 14%
where the time goes in v3:
time: 125 us; the launch traced here: 124 us
  starting transfers between devices  41.4 us (33%)
  waiting for transfers between devices  34.1 us (27%)
  Pallas kernels  25.4 us (20%)
  blocking collectives  17.1 us (14%)
  local copies, waits for them, and re-layouts  3.81 us (3%)
  between operations  1.44 us (1%)
    all_to_all x1, blocking collectives, local(): fetched = lax.all_to_all(picked, 'ent', 0, 0, tiled=True)  17.1 us
    ppermute x12, starting transfers between devices, ring(): lax.ppermute(x, 'rel', [((k + shift) % n_rel, k) for k in range(n_rel)])  16.4 us
    all_to_all x1, waiting for transfers between devices, local(): returned = lax.all_to_all(packed, 'ent', 0, 0, tiled=True)  14.5 us
    all_to_all x1, starting transfers between devices, local(): lax.all_to_all(request_rows.reshape(parts, 1, slots), 'ent', 0, 0, tiled=...  13.1 us
    ppermute x12, waiting for transfers between devices, ring(): lax.ppermute(x, 'rel', [((k + shift) % n_rel, k) for k in range(n_rel)])  11.7 us
    pallas_call x1, Pallas kernels, local(): pl.pallas_call(functools.partial(head_kernel, r_count, blocks), grid=(ste...  7.85 us
    all_to_all x1, waiting for transfers between devices, local(): lax.all_to_all(request_rows.reshape(parts, 1, slots), 'ent', 0, 0, tiled=...  7.52 us
    pallas_call x1, Pallas kernels, local(): pl.pallas_call(functools.partial(grad_kernel, blocks), grid=(r_count,), i...  6.92 us
  transfers between devices with their start and end apart: 15, of which 8 were waited for; matrix products, arithmetic and copies ran while one was open for 1% of the time, Pallas kernels for 14%

profile of v3, /device:TPU:1, one launch (start us, length us, event | category | flops | bytes accessed | tf_op | source)
XLA Modules:
  0.0 124.3 jit_solution(16602111409510119565)
XLA Ops:
  0.6 1.4 %copy.11 = s32[1,64,32]{2,1,0:T(8,128)} copy(s32[1,64,32]{1,2,0:T(8,128)} %param.9) | data formatting | bytes 16384 | tf_op args[1]
  2.0 13.1 %all-to-all-start = ((s32[64,1,32]{2,1,0:T(1,128)}), s32[64,1,32]{2,1,0:T(1,128)S(1)}, u32[]{:S(2)}, u32[]{:S(2)}) async-start(s32[64,1,32]{2,1,0:T(1,128)} %bitcast.6), calls=%async_computation | async-start | bytes 65536 | tf_op jit(solution)/shard_map/all_to_all | solution.py:249
  17.0 7.5 %all-to-all-done = s32[64,1,32]{2,1,0:T(1,128)S(1)} async-done(((s32[64,1,32]{2,1,0:T(1,128)}), s32[64,1,32]{2,1,0:T(1,128)S(1)}, u32[]{:S(2)}, u32[]{:S(2)}) %all-to-all-start) | async-done | bytes 8224 | tf_op jit(solution)/shard_map/all_to_all | solution.py:249
  24.5 1.1 pick.1
  25.6 17.1 %all_to_all.36 = bf16[64,8,256]{2,1,0:T(8,128)(2,1)S(1)} all-to-all(bf16[64,8,256]{2,1,0:T(8,128)(2,1)S(1)} %bitcast.27), channel_id=1, replica_groups=mesh['ent'=64,'rel'=4] {'ent'}, dimensions={0} | all-to-all | bytes 524288 | tf_op jit(solution)/shard_map/all_to_all | solution.py:298
  42.7 1.2 collective-permute-start.2
  43.9 2.5 %collective-permute-start.1 = (bf16[512,256]{1,0:T(8,128)(2,1)S(1)}, bf16[512,256]{1,0:T(8,128)(2,1)S(1)}, u32[]{:S(2)}, u32[]{:S(2)}) collective-permute-start(bf16[512,256]{1,0:T(8,128)(2,1)S(1)} %bitcast.24), channel_id=1, source_target_pairs={{2,0},{3,1},{0,2},{1,3},{6,4},{7,5},{4,6},{5,7},{10,8},{11,9},{8,1... | collective-permute-start | bytes 786440 | tf_op jit(solution)/shard_map/ppermute | solution.py:230
  46.3 1.2 collective-permute-start
  48.2 7.8 %head_step.1 = (bf16[1024,256]{1,0:T(8,128)(2,1)S(1)}, f32[1024,256]{1,0:T(8,128)S(1)}, bf16[256,1024]{1,0:T(8,128)(2,1)S(1)}, f32[1024,256]{1,0:T(8,128)S(1)}, bf16[2048,256]{1,0:T(8,128)(2,1)S(1)}) custom-call(s32[2]{0:T(128)S(1)} %pad_add_fusion.scal, s32[4,1,256]{2,1,0:T(1,128)S(1)} %bitcast.32, s32[4,1,256]{2,1,0:T(1,128)S(1)} %bitcast.34, ...), custom_call_target="tpu_custom_call" | custom-call | flops 3000000000 | bytes 6000000 | tf_op jit(solution)/shard_map/head_step/pallas_call | solution.py:277
  56.1 2.0 %collective-permute-done.1.refs_2_ = bf16[512,256]{1,0:T(8,128)(2,1)S(1)} collective-permute-done((bf16[512,256]{1,0:T(8,128)(2,1)S(1)}, bf16[512,256]{1,0:T(8,128)(2,1)S(1)}, u32[]{:S(2)}, u32[]{:S(2)}) %collective-permute-start.1) | collective-permute-done | bytes 262176 | tf_op jit(solution)/shard_map/ppermute | solution.py:230
  58.1 4.9 %tail_step.1 = (bf16[1024,256]{1,0:T(8,128)(2,1)S(1)}, bf16[512,256]{1,0:T(8,128)(2,1)S(1)}, bf16[512,256]{1,0:T(8,128)(2,1)S(1)}, bf16[512,256]{1,0:T(8,128)(2,1)S(1)}, bf16[512,256]{1,0:T(8,128)(2,1)S(1)}) custom-call(s32[2]{0:T(128)S(1)} %pad_add_fusion.scal, s32[4,1,256]{2,1,0:T(1,128)S(1)} %bitcast.31, bf16[1024,256]{1,0:T(8,128)(2,1)S(1)} %get-tuple-element.20.proj, ...), custom_call_target="tpu_custom_call" | custom-call | flops 3000000000 | bytes 5000000 | tf_op jit(solution)/shard_map/tail_step/pallas_call | solution.py:301
  63.0 1.1 collective-permute-start.3
  64.1 2.8 %collective-permute-start.4 = (bf16[512,256]{1,0:T(8,128)(2,1)S(1)}, bf16[512,256]{1,0:T(8,128)(2,1)S(1)}, u32[]{:S(2)}, u32[]{:S(2)}) collective-permute-start(bf16[512,256]{1,0:T(8,128)(2,1)S(1)} %get-tuple-element.24), channel_id=1, source_target_pairs={{2,0},{3,1},{0,2},{1,3},{6,4},{7,5},{4,6},{5,7},{10,8},{11,9},{8,1... | collective-permute-start | bytes 786440 | tf_op jit(solution)/shard_map/ppermute | solution.py:230
  67.3 6.9 %grad_step.1 = (bf16[512,128]{1,0:T(8,128)(2,1)S(1)}, f32[1024,256]{1,0:T(8,128)S(1)}) custom-call(s32[1,1024]{1,0:T(1,128)S(1)} %bitcast.33, s32[1,1024]{1,0:T(1,128)S(1)} %bitcast.35, bf16[1024,256]{1,0:T(8,128)(2,1)S(1)} %get-tuple-element.26.gp.after, bf16[256,1024]{1,0:T(8,128)(2,1)S(1)} %get-tuple-element.27.turned, ...), custom_call_target="tpu_custom_call" | custom-call | flops 3000000000 | bytes 6000000 | tf_op jit(solution)/shard_map/grad_step/pallas_call | solution.py:325
  74.3 4.2 %collective-permute-done.4 = bf16[512,256]{1,0:T(8,128)(2,1)S(1)} collective-permute-done((bf16[512,256]{1,0:T(8,128)(2,1)S(1)}, bf16[512,256]{1,0:T(8,128)(2,1)S(1)}, u32[]{:S(2)}, u32[]{:S(2)}) %collective-permute-start.4) | collective-permute-done | bytes 262176 | tf_op jit(solution)/shard_map/ppermute | solution.py:230
  79.4 5.6 %all-to-all-start.2 = ((bf16[64,8,384]{2,1,0:T(8,128)(2,1)}), bf16[64,8,384]{2,1,0:T(8,128)(2,1)S(1)}, u32[]{:S(2)}, u32[]{:S(2)}) async-start(bf16[64,8,384]{2,1,0:T(8,128)(2,1)} %maximum_bitcast_fusion), calls=%async_computation.2 | async-start | bytes 786432 | tf_op jit(solution)/shard_map/all_to_all | solution.py:341
  85.8 14.5 %all-to-all-done.2 = bf16[64,8,384]{2,1,0:T(8,128)(2,1)S(1)} async-done(((bf16[64,8,384]{2,1,0:T(8,128)(2,1)}), bf16[64,8,384]{2,1,0:T(8,128)(2,1)S(1)}, u32[]{:S(2)}, u32[]{:S(2)}) %all-to-all-start.2) | async-done | bytes 393248 | tf_op jit(solution)/shard_map/all_to_all | solution.py:341
  102.3 2.1 %collective-permute-start.7 = (bf16[256,256]{1,0:T(8,128)(2,1)S(1)}, bf16[256,256]{1,0:T(8,128)(2,1)S(1)}, u32[]{:S(2)}, u32[]{:S(2)}) collective-permute-start(bf16[256,256]{1,0:T(8,128)(2,1)S(1)} %get-tuple-element.34), channel_id=1, source_target_pairs={{2,0},{3,1},{0,2},{1,3},{6,4},{7,5},{4,6},{5,7},{10,8},{11,9},{8,1... | collective-permute-start | bytes 393224 | tf_op jit(solution)/shard_map/ppermute | solution.py:230
  105.8 6.2 %all-to-all-start.3 = ((bf16[64,8,128]{2,1,0:T(8,128)(2,1)}), bf16[64,8,128]{2,1,0:T(8,128)(2,1)S(1)}, u32[]{:S(2)}, u32[]{:S(2)}) async-start(bf16[64,8,128]{2,1,0:T(8,128)(2,1)} %broadcast_in_dim.2), calls=%async_computation.3 | async-start | bytes 262144 | tf_op jit(solution)/shard_map/all_to_all | solution.py:344
  113.1 2.0 %collective-permute-start.10 = (bf16[256,256]{1,0:T(8,128)(2,1)S(1)}, bf16[256,256]{1,0:T(8,128)(2,1)S(1)}, u32[]{:S(2)}, u32[]{:S(2)}) collective-permute-start(bf16[256,256]{1,0:T(8,128)(2,1)S(1)} %add_convert_fusion.1.refs_0_), channel_id=1, source_target_pairs={{2,0},{3,1},{0,2},{1,3},{6,4},{7,5},{4,6},{5,7},{10,8},{11,9},{8,1... | collective-permute-start | bytes 393224 | tf_op jit(solution)/shard_map/ppermute | solution.py:230
  115.7 2.4 %collective-permute-done.11.refs_3_ = bf16[256,256]{1,0:T(8,128)(2,1)S(1)} collective-permute-done((bf16[256,256]{1,0:T(8,128)(2,1)S(1)}, bf16[256,256]{1,0:T(8,128)(2,1)S(1)}, u32[]{:S(2)}, u32[]{:S(2)}) %collective-permute-start.11) | collective-permute-done | bytes 131104 | tf_op jit(solution)/shard_map/ppermute | solution.py:230
  118.1 2.9 %collective-permute-done.10.refs_2_ = bf16[256,256]{1,0:T(8,128)(2,1)S(1)} collective-permute-done((bf16[256,256]{1,0:T(8,128)(2,1)S(1)}, bf16[256,256]{1,0:T(8,128)(2,1)S(1)}, u32[]{:S(2)}, u32[]{:S(2)}) %collective-permute-start.10) | collective-permute-done | bytes 131104 | tf_op jit(solution)/shard_map/ppermute | solution.py:230
  121.2 1.6 %place_rows.1 = f32[1024,256]{1,0:T(8,128)} custom-call(s32[2]{0:T(128)S(1)} %pad_add_fusion.scal, bf16[256,256]{1,0:T(8,128)(2,1)S(1)} %add_convert_fusion.1.refs_0_, bf16[256,256]{1,0:T(8,128)(2,1)S(1)} %collective-permute-done.9.refs_1_, bf16[256,256]{1,0:T(8,128)(2,1)S(1)} %collective-permute-done.10.refs_2_, ...), custom_call_target="tpu_custom_call" | custom-call | flops 1000000 | bytes 1500000 | tf_op jit(solution)/shard_map/place_rows/pallas_call | solution.py:360
  123.2 1.1 relation_out.1
  (37 shorter events, 9.5 us)
Async XLA Ops:
  2.0 22.5 %all-to-all-start = ((s32[64,1,32]{2,1,0:T(1,128)}), s32[64,1,32]{2,1,0:T(1,128)S(1)}, u32[]{:S(2)}, u32[]{:S(2)}) async-start(s32[64,1,32]{2,1,0:T(1,128)} %bitcast.6), calls=%async_computation | async-start | bytes 65536 | tf_op jit(solution)/shard_map/all_to_all | solution.py:249
  15.9 1.0 copy-start
  24.5 23.0 %copy-start.1 = (bf16[1024,256]{1,0:T(8,128)(2,1)S(1)}, bf16[1024,256]{1,0:T(8,128)(2,1)}, u32[]{:S(2)}) copy-start(bf16[1024,256]{1,0:T(8,128)(2,1)} %table.3) | copy-start | bytes 1572868
  24.5 23.0 %copy-start.2 = (bf16[8,8,32,32]{3,2,1,0:T(8,128)(2,1)S(1)}, bf16[8,8,32,32]{3,2,1,0:T(8,128)(2,1)}, u32[]{:S(2)}) copy-start(bf16[8,8,32,32]{3,2,1,0:T(8,128)(2,1)} %param.15) | copy-start | bytes 393220
  42.7 4.8 %copy-start.5 = (s32[1024]{0:T(1024)S(1)}, s32[1024]{0:T(1024)}, u32[]{:S(2)}) copy-start(s32[1024]{0:T(1024)} %param.11) | copy-start | bytes 12292
  42.7 4.8 %copy-start.4 = (s32[1024]{0:T(1024)S(1)}, s32[1024]{0:T(1024)}, u32[]{:S(2)}) copy-start(s32[1024]{0:T(1024)} %param.10) | copy-start | bytes 12292
  42.7 13.4 %collective-permute-start.2 = (bf16[512,256]{1,0:T(8,128)(2,1)S(1)}, bf16[512,256]{1,0:T(8,128)(2,1)S(1)}, u32[]{:S(2)}, u32[]{:S(2)}) collective-permute-start(bf16[512,256]{1,0:T(8,128)(2,1)S(1)} %bitcast.23), channel_id=1, source_target_pairs={{3,0},{0,1},{1,2},{2,3},{7,4},{4,5},{5,6},{6,7},{11,8},{8,9},{9,10... | collective-permute-start | bytes 786440 | tf_op jit(solution)/shard_map/ppermute | solution.py:230
  43.9 14.2 %collective-permute-start.1 = (bf16[512,256]{1,0:T(8,128)(2,1)S(1)}, bf16[512,256]{1,0:T(8,128)(2,1)S(1)}, u32[]{:S(2)}, u32[]{:S(2)}) collective-permute-start(bf16[512,256]{1,0:T(8,128)(2,1)S(1)} %bitcast.24), channel_id=1, source_target_pairs={{2,0},{3,1},{0,2},{1,3},{6,4},{7,5},{4,6},{5,7},{10,8},{11,9},{8,1... | collective-permute-start | bytes 786440 | tf_op jit(solution)/shard_map/ppermute | solution.py:230
  46.3 11.7 %collective-permute-start = (bf16[512,256]{1,0:T(8,128)(2,1)S(1)}, bf16[512,256]{1,0:T(8,128)(2,1)S(1)}, u32[]{:S(2)}, u32[]{:S(2)}) collective-permute-start(bf16[512,256]{1,0:T(8,128)(2,1)S(1)} %bitcast.25), channel_id=1, source_target_pairs={{1,0},{2,1},{3,2},{0,3},{5,4},{6,5},{7,6},{4,7},{9,8},{10,9},{11,1... | collective-permute-start | bytes 786440 | tf_op jit(solution)/shard_map/ppermute | solution.py:230
  47.5 0.7 copy-start.6
  56.0 2.1 %copy-start.3 = (s32[1024]{0:T(1024)S(1)}, s32[1024]{0:T(1024)}, u32[]{:S(2)}) copy-start(s32[1024]{0:T(1024)} %param.12) | copy-start | bytes 12292
  63.0 11.2 %collective-permute-start.3 = (bf16[512,256]{1,0:T(8,128)(2,1)S(1)}, bf16[512,256]{1,0:T(8,128)(2,1)S(1)}, u32[]{:S(2)}, u32[]{:S(2)}) collective-permute-start(bf16[512,256]{1,0:T(8,128)(2,1)S(1)} %get-tuple-element.23), channel_id=1, source_target_pairs={{3,0},{0,1},{1,2},{2,3},{7,4},{4,5},{5,6},{6,7},{11,8},{8,9},{9,10... | collective-permute-start | bytes 786440 | tf_op jit(solution)/shard_map/ppermute | solution.py:230
  64.1 14.3 %collective-permute-start.4 = (bf16[512,256]{1,0:T(8,128)(2,1)S(1)}, bf16[512,256]{1,0:T(8,128)(2,1)S(1)}, u32[]{:S(2)}, u32[]{:S(2)}) collective-permute-start(bf16[512,256]{1,0:T(8,128)(2,1)S(1)} %get-tuple-element.24), channel_id=1, source_target_pairs={{2,0},{3,1},{0,2},{1,3},{6,4},{7,5},{4,6},{5,7},{10,8},{11,9},{8,1... | collective-permute-start | bytes 786440 | tf_op jit(solution)/shard_map/ppermute | solution.py:230
  66.9 11.5 %collective-permute-start.5 = (bf16[512,256]{1,0:T(8,128)(2,1)S(1)}, bf16[512,256]{1,0:T(8,128)(2,1)S(1)}, u32[]{:S(2)}, u32[]{:S(2)}) collective-permute-start(bf16[512,256]{1,0:T(8,128)(2,1)S(1)} %get-tuple-element.25), channel_id=1, source_target_pairs={{1,0},{2,1},{3,2},{0,3},{5,4},{6,5},{7,6},{4,7},{9,8},{10,9},{11,1... | collective-permute-start | bytes 786440 | tf_op jit(solution)/shard_map/ppermute | solution.py:230
  79.4 20.9 %all-to-all-start.2 = ((bf16[64,8,384]{2,1,0:T(8,128)(2,1)}), bf16[64,8,384]{2,1,0:T(8,128)(2,1)S(1)}, u32[]{:S(2)}, u32[]{:S(2)}) async-start(bf16[64,8,384]{2,1,0:T(8,128)(2,1)} %maximum_bitcast_fusion), calls=%async_computation.2 | async-start | bytes 786432 | tf_op jit(solution)/shard_map/all_to_all | solution.py:341
  101.3 10.8 %collective-permute-start.6 = (bf16[256,256]{1,0:T(8,128)(2,1)S(1)}, bf16[256,256]{1,0:T(8,128)(2,1)S(1)}, u32[]{:S(2)}, u32[]{:S(2)}) collective-permute-start(bf16[256,256]{1,0:T(8,128)(2,1)S(1)} %get-tuple-element.33), channel_id=1, source_target_pairs={{3,0},{0,1},{1,2},{2,3},{7,4},{4,5},{5,6},{6,7},{11,8},{8,9},{9,10... | collective-permute-start | bytes 393224 | tf_op jit(solution)/shard_map/ppermute | solution.py:230
  102.3 9.8 %collective-permute-start.7 = (bf16[256,256]{1,0:T(8,128)(2,1)S(1)}, bf16[256,256]{1,0:T(8,128)(2,1)S(1)}, u32[]{:S(2)}, u32[]{:S(2)}) collective-permute-start(bf16[256,256]{1,0:T(8,128)(2,1)S(1)} %get-tuple-element.34), channel_id=1, source_target_pairs={{2,0},{3,1},{0,2},{1,3},{6,4},{7,5},{4,6},{5,7},{10,8},{11,9},{8,1... | collective-permute-start | bytes 393224 | tf_op jit(solution)/shard_map/ppermute | solution.py:230
  104.4 7.7 %collective-permute-start.8 = (bf16[256,256]{1,0:T(8,128)(2,1)S(1)}, bf16[256,256]{1,0:T(8,128)(2,1)S(1)}, u32[]{:S(2)}, u32[]{:S(2)}) collective-permute-start(bf16[256,256]{1,0:T(8,128)(2,1)S(1)} %get-tuple-element.35), channel_id=1, source_target_pairs={{1,0},{2,1},{3,2},{0,3},{5,4},{6,5},{7,6},{4,7},{9,8},{10,9},{11,1... | collective-permute-start | bytes 393224 | tf_op jit(solution)/shard_map/ppermute | solution.py:230
  105.8 17.3 %all-to-all-start.3 = ((bf16[64,8,128]{2,1,0:T(8,128)(2,1)}), bf16[64,8,128]{2,1,0:T(8,128)(2,1)S(1)}, u32[]{:S(2)}, u32[]{:S(2)}) async-start(bf16[64,8,128]{2,1,0:T(8,128)(2,1)} %broadcast_in_dim.2), calls=%async_computation.3 | async-start | bytes 262144 | tf_op jit(solution)/shard_map/all_to_all | solution.py:344
  112.2 5.9 %collective-permute-start.11 = (bf16[256,256]{1,0:T(8,128)(2,1)S(1)}, bf16[256,256]{1,0:T(8,128)(2,1)S(1)}, u32[]{:S(2)}, u32[]{:S(2)}) collective-permute-start(bf16[256,256]{1,0:T(8,128)(2,1)S(1)} %add_convert_fusion.1.refs_0_), channel_id=1, source_target_pairs={{3,0},{0,1},{1,2},{2,3},{7,4},{4,5},{5,6},{6,7},{11,8},{8,9},{9,10... | collective-permute-start | bytes 393224 | tf_op jit(solution)/shard_map/ppermute | solution.py:230
  113.1 7.9 %collective-permute-start.10 = (bf16[256,256]{1,0:T(8,128)(2,1)S(1)}, bf16[256,256]{1,0:T(8,128)(2,1)S(1)}, u32[]{:S(2)}, u32[]{:S(2)}) collective-permute-start(bf16[256,256]{1,0:T(8,128)(2,1)S(1)} %add_convert_fusion.1.refs_0_), channel_id=1, source_target_pairs={{2,0},{3,1},{0,2},{1,3},{6,4},{7,5},{4,6},{5,7},{10,8},{11,9},{8,1... | collective-permute-start | bytes 393224 | tf_op jit(solution)/shard_map/ppermute | solution.py:230
  115.1 6.1 %collective-permute-start.9 = (bf16[256,256]{1,0:T(8,128)(2,1)S(1)}, bf16[256,256]{1,0:T(8,128)(2,1)S(1)}, u32[]{:S(2)}, u32[]{:S(2)}) collective-permute-start(bf16[256,256]{1,0:T(8,128)(2,1)S(1)} %add_convert_fusion.1.refs_0_), channel_id=1, source_target_pairs={{1,0},{2,1},{3,2},{0,3},{5,4},{6,5},{7,6},{4,7},{9,8},{10,9},{11,1... | collective-permute-start | bytes 393224 | tf_op jit(solution)/shard_map/ppermute | solution.py:230

commit v4 on v3

--- a/solution.py
+++ b/solution.py
@@ -9,7 +9,7 @@
 
 F32 = jnp.float32
 BF16 = jnp.bfloat16
-TILE = 256
+TILE = 512
 SMEM = pl.BlockSpec(memory_space=pltpu.SMEM)
 ANY = pl.BlockSpec(memory_space=pl.ANY)
 CONTRACT_LAST = (((1,), (1,)), ((), ()))

time: 125 us -> 124 us (level)
  Pallas kernels: 25.4 us -> 22.7 us
  waiting for transfers between devices: 34.1 us -> 35.5 us
    ppermute x12, waiting for transfers between devices: 11.7 us -> 13.3 us  [ring(): lax.ppermute(x, 'rel', [((k + shift) % n_rel, k) for k in range(n_rel)])]
    pallas_call x1, Pallas kernels: 7.85 us -> 6.4 us  [local(): pl.pallas_call(functools.partial(head_kernel, r_count, blocks), grid=(ste...]
  transfers between devices with their start and end apart: 15 -> 15, of which waited for: 8 -> 8; matrix products, arithmetic and copies ran while one was open for 1% -> 1% of each run, Pallas kernels for 14% -> 13%
where the time goes in v4:
time: 124 us; the launch traced here: 123 us
  starting transfers between devices  41.4 us (33%)
  waiting for transfers between devices  35.5 us (29%)
  Pallas kernels  22.7 us (18%)
  blocking collectives  17.1 us (14%)
  local copies, waits for them, and re-layouts  3.81 us (3%)
  between operations  1.44 us (1%)
    all_to_all x1, blocking collectives, local(): fetched = lax.all_to_all(picked, 'ent', 0, 0, tiled=True)  17.1 us
    ppermute x12, starting transfers between devices, ring(): lax.ppermute(x, 'rel', [((k + shift) % n_rel, k) for k in range(n_rel)])  16.3 us
    all_to_all x1, waiting for transfers between devices, local(): returned = lax.all_to_all(packed, 'ent', 0, 0, tiled=True)  14.3 us
    ppermute x12, waiting for transfers between devices, ring(): lax.ppermute(x, 'rel', [((k + shift) % n_rel, k) for k in range(n_rel)])  13.3 us
    all_to_all x1, starting transfers between devices, local(): lax.all_to_all(request_rows.reshape(parts, 1, slots), 'ent', 0, 0, tiled=...  13.1 us
    all_to_all x1, waiting for transfers between devices, local(): lax.all_to_all(request_rows.reshape(parts, 1, slots), 'ent', 0, 0, tiled=...  7.52 us
    pallas_call x1, Pallas kernels, local(): pl.pallas_call(functools.partial(grad_kernel, blocks), grid=(r_count,), i...  6.71 us
    pallas_call x1, Pallas kernels, local(): pl.pallas_call(functools.partial(head_kernel, r_count, blocks), grid=(ste...  6.4 us
  transfers between devices with their start and end apart: 15, of which 8 were waited for; matrix products, arithmetic and copies ran while one was open for 1% of the time, Pallas kernels for 13%

profile of v4, /device:TPU:1, one launch (start us, length us, event | category | flops | bytes accessed | tf_op | source)
XLA Modules:
  0.0 123.1 jit_solution(3334395171780928688)
XLA Ops:
  0.6 1.4 %copy.11 = s32[1,64,32]{2,1,0:T(8,128)} copy(s32[1,64,32]{1,2,0:T(8,128)} %param.9) | data formatting | bytes 16384 | tf_op args[1]
  2.0 13.1 %all-to-all-start = ((s32[64,1,32]{2,1,0:T(1,128)}), s32[64,1,32]{2,1,0:T(1,128)S(1)}, u32[]{:S(2)}, u32[]{:S(2)}) async-start(s32[64,1,32]{2,1,0:T(1,128)} %bitcast.6), calls=%async_computation | async-start | bytes 65536 | tf_op jit(solution)/shard_map/all_to_all | solution.py:249
  17.0 7.5 %all-to-all-done = s32[64,1,32]{2,1,0:T(1,128)S(1)} async-done(((s32[64,1,32]{2,1,0:T(1,128)}), s32[64,1,32]{2,1,0:T(1,128)S(1)}, u32[]{:S(2)}, u32[]{:S(2)}) %all-to-all-start) | async-done | bytes 8224 | tf_op jit(solution)/shard_map/all_to_all | solution.py:249
  24.5 1.1 pick.1
  25.6 17.1 %all_to_all.36 = bf16[64,8,256]{2,1,0:T(8,128)(2,1)S(1)} all-to-all(bf16[64,8,256]{2,1,0:T(8,128)(2,1)S(1)} %bitcast.27), channel_id=1, replica_groups=mesh['ent'=64,'rel'=4] {'ent'}, dimensions={0} | all-to-all | bytes 524288 | tf_op jit(solution)/shard_map/all_to_all | solution.py:298
  42.7 1.2 collective-permute-start.2
  43.9 2.5 %collective-permute-start.1 = (bf16[512,256]{1,0:T(8,128)(2,1)S(1)}, bf16[512,256]{1,0:T(8,128)(2,1)S(1)}, u32[]{:S(2)}, u32[]{:S(2)}) collective-permute-start(bf16[512,256]{1,0:T(8,128)(2,1)S(1)} %bitcast.24), channel_id=1, source_target_pairs={{2,0},{3,1},{0,2},{1,3},{6,4},{7,5},{4,6},{5,7},{10,8},{11,9},{8,1... | collective-permute-start | bytes 786440 | tf_op jit(solution)/shard_map/ppermute | solution.py:230
  46.3 1.2 collective-permute-start
  48.2 6.4 %head_step.1 = (bf16[1024,256]{1,0:T(8,128)(2,1)S(1)}, f32[1024,256]{1,0:T(8,128)S(1)}, bf16[256,1024]{1,0:T(8,128)(2,1)S(1)}, f32[1024,256]{1,0:T(8,128)S(1)}, bf16[2048,256]{1,0:T(8,128)(2,1)S(1)}) custom-call(s32[2]{0:T(128)S(1)} %pad_add_fusion.scal, s32[2,1,512]{2,1,0:T(1,128)S(1)} %bitcast.32, s32[2,1,512]{2,1,0:T(1,128)S(1)} %bitcast.34, ...), custom_call_target="tpu_custom_call" | custom-call | flops 3000000000 | bytes 6000000 | tf_op jit(solution)/shard_map/head_step/pallas_call | solution.py:277
  54.6 3.5 %collective-permute-done.1.refs_2_ = bf16[512,256]{1,0:T(8,128)(2,1)S(1)} collective-permute-done((bf16[512,256]{1,0:T(8,128)(2,1)S(1)}, bf16[512,256]{1,0:T(8,128)(2,1)S(1)}, u32[]{:S(2)}, u32[]{:S(2)}) %collective-permute-start.1) | collective-permute-done | bytes 262176 | tf_op jit(solution)/shard_map/ppermute | solution.py:230
  58.1 4.0 %tail_step.1 = (bf16[1024,256]{1,0:T(8,128)(2,1)S(1)}, bf16[512,256]{1,0:T(8,128)(2,1)S(1)}, bf16[512,256]{1,0:T(8,128)(2,1)S(1)}, bf16[512,256]{1,0:T(8,128)(2,1)S(1)}, bf16[512,256]{1,0:T(8,128)(2,1)S(1)}) custom-call(s32[2]{0:T(128)S(1)} %pad_add_fusion.scal, s32[2,1,512]{2,1,0:T(1,128)S(1)} %bitcast.31, bf16[1024,256]{1,0:T(8,128)(2,1)S(1)} %get-tuple-element.20.proj, ...), custom_call_target="tpu_custom_call" | custom-call | flops 3000000000 | bytes 5000000 | tf_op jit(solution)/shard_map/tail_step/pallas_call | solution.py:301
  62.1 1.1 collective-permute-start.3
  63.2 2.8 %collective-permute-start.4 = (bf16[512,256]{1,0:T(8,128)(2,1)S(1)}, bf16[512,256]{1,0:T(8,128)(2,1)S(1)}, u32[]{:S(2)}, u32[]{:S(2)}) collective-permute-start(bf16[512,256]{1,0:T(8,128)(2,1)S(1)} %get-tuple-element.24), channel_id=1, source_target_pairs={{2,0},{3,1},{0,2},{1,3},{6,4},{7,5},{4,6},{5,7},{10,8},{11,9},{8,1... | collective-permute-start | bytes 786440 | tf_op jit(solution)/shard_map/ppermute | solution.py:230
  66.4 6.7 %grad_step.1 = (bf16[512,128]{1,0:T(8,128)(2,1)S(1)}, f32[1024,256]{1,0:T(8,128)S(1)}) custom-call(s32[1,1024]{1,0:T(1,128)S(1)} %bitcast.33, s32[1,1024]{1,0:T(1,128)S(1)} %bitcast.35, bf16[1024,256]{1,0:T(8,128)(2,1)S(1)} %get-tuple-element.26.gp.after, bf16[256,1024]{1,0:T(8,128)(2,1)S(1)} %get-tuple-element.27.turned, ...), custom_call_target="tpu_custom_call" | custom-call | flops 3000000000 | bytes 6000000 | tf_op jit(solution)/shard_map/grad_step/pallas_call | solution.py:325
  73.1 4.4 %collective-permute-done.4 = bf16[512,256]{1,0:T(8,128)(2,1)S(1)} collective-permute-done((bf16[512,256]{1,0:T(8,128)(2,1)S(1)}, bf16[512,256]{1,0:T(8,128)(2,1)S(1)}, u32[]{:S(2)}, u32[]{:S(2)}) %collective-permute-start.4) | collective-permute-done | bytes 262176 | tf_op jit(solution)/shard_map/ppermute | solution.py:230
  78.4 5.6 %all-to-all-start.2 = ((bf16[64,8,384]{2,1,0:T(8,128)(2,1)}), bf16[64,8,384]{2,1,0:T(8,128)(2,1)S(1)}, u32[]{:S(2)}, u32[]{:S(2)}) async-start(bf16[64,8,384]{2,1,0:T(8,128)(2,1)} %maximum_bitcast_fusion), calls=%async_computation.2 | async-start | bytes 786432 | tf_op jit(solution)/shard_map/all_to_all | solution.py:341
  84.9 14.3 %all-to-all-done.2 = bf16[64,8,384]{2,1,0:T(8,128)(2,1)S(1)} async-done(((bf16[64,8,384]{2,1,0:T(8,128)(2,1)}), bf16[64,8,384]{2,1,0:T(8,128)(2,1)S(1)}, u32[]{:S(2)}, u32[]{:S(2)}) %all-to-all-start.2) | async-done | bytes 393248 | tf_op jit(solution)/shard_map/all_to_all | solution.py:341
  101.1 2.2 %collective-permute-start.7 = (bf16[256,256]{1,0:T(8,128)(2,1)S(1)}, bf16[256,256]{1,0:T(8,128)(2,1)S(1)}, u32[]{:S(2)}, u32[]{:S(2)}) collective-permute-start(bf16[256,256]{1,0:T(8,128)(2,1)S(1)} %get-tuple-element.34), channel_id=1, source_target_pairs={{2,0},{3,1},{0,2},{1,3},{6,4},{7,5},{4,6},{5,7},{10,8},{11,9},{8,1... | collective-permute-start | bytes 393224 | tf_op jit(solution)/shard_map/ppermute | solution.py:230
  104.6 6.3 %all-to-all-start.3 = ((bf16[64,8,128]{2,1,0:T(8,128)(2,1)}), bf16[64,8,128]{2,1,0:T(8,128)(2,1)S(1)}, u32[]{:S(2)}, u32[]{:S(2)}) async-start(bf16[64,8,128]{2,1,0:T(8,128)(2,1)} %broadcast_in_dim.2), calls=%async_computation.3 | async-start | bytes 262144 | tf_op jit(solution)/shard_map/all_to_all | solution.py:344
  112.0 2.0 %collective-permute-start.10 = (bf16[256,256]{1,0:T(8,128)(2,1)S(1)}, bf16[256,256]{1,0:T(8,128)(2,1)S(1)}, u32[]{:S(2)}, u32[]{:S(2)}) collective-permute-start(bf16[256,256]{1,0:T(8,128)(2,1)S(1)} %add_convert_fusion.1.refs_0_), channel_id=1, source_target_pairs={{2,0},{3,1},{0,2},{1,3},{6,4},{7,5},{4,6},{5,7},{10,8},{11,9},{8,1... | collective-permute-start | bytes 393224 | tf_op jit(solution)/shard_map/ppermute | solution.py:230
  114.6 2.3 %collective-permute-done.11.refs_3_ = bf16[256,256]{1,0:T(8,128)(2,1)S(1)} collective-permute-done((bf16[256,256]{1,0:T(8,128)(2,1)S(1)}, bf16[256,256]{1,0:T(8,128)(2,1)S(1)}, u32[]{:S(2)}, u32[]{:S(2)}) %collective-permute-start.11) | collective-permute-done | bytes 131104 | tf_op jit(solution)/shard_map/ppermute | solution.py:230
  116.9 3.0 %collective-permute-done.10.refs_2_ = bf16[256,256]{1,0:T(8,128)(2,1)S(1)} collective-permute-done((bf16[256,256]{1,0:T(8,128)(2,1)S(1)}, bf16[256,256]{1,0:T(8,128)(2,1)S(1)}, u32[]{:S(2)}, u32[]{:S(2)}) %collective-permute-start.10) | collective-permute-done | bytes 131104 | tf_op jit(solution)/shard_map/ppermute | solution.py:230
  120.0 1.6 %place_rows.1 = f32[1024,256]{1,0:T(8,128)} custom-call(s32[2]{0:T(128)S(1)} %pad_add_fusion.scal, bf16[256,256]{1,0:T(8,128)(2,1)S(1)} %add_convert_fusion.1.refs_0_, bf16[256,256]{1,0:T(8,128)(2,1)S(1)} %collective-permute-done.9.refs_1_, bf16[256,256]{1,0:T(8,128)(2,1)S(1)} %collective-permute-done.10.refs_2_, ...), custom_call_target="tpu_custom_call" | custom-call | flops 1000000 | bytes 1500000 | tf_op jit(solution)/shard_map/place_rows/pallas_call | solution.py:360
  122.0 1.1 relation_out.1
  (37 shorter events, 9.4 us)
Async XLA Ops:
  2.0 22.5 %all-to-all-start = ((s32[64,1,32]{2,1,0:T(1,128)}), s32[64,1,32]{2,1,0:T(1,128)S(1)}, u32[]{:S(2)}, u32[]{:S(2)}) async-start(s32[64,1,32]{2,1,0:T(1,128)} %bitcast.6), calls=%async_computation | async-start | bytes 65536 | tf_op jit(solution)/shard_map/all_to_all | solution.py:249
  15.9 1.0 copy-start
  24.5 23.0 %copy-start.1 = (bf16[1024,256]{1,0:T(8,128)(2,1)S(1)}, bf16[1024,256]{1,0:T(8,128)(2,1)}, u32[]{:S(2)}) copy-start(bf16[1024,256]{1,0:T(8,128)(2,1)} %table.3) | copy-start | bytes 1572868
  24.5 23.0 %copy-start.2 = (bf16[8,8,32,32]{3,2,1,0:T(8,128)(2,1)S(1)}, bf16[8,8,32,32]{3,2,1,0:T(8,128)(2,1)}, u32[]{:S(2)}) copy-start(bf16[8,8,32,32]{3,2,1,0:T(8,128)(2,1)} %param.15) | copy-start | bytes 393220
  42.7 4.8 %copy-start.5 = (s32[1024]{0:T(1024)S(1)}, s32[1024]{0:T(1024)}, u32[]{:S(2)}) copy-start(s32[1024]{0:T(1024)} %param.11) | copy-start | bytes 12292
  42.7 4.8 %copy-start.4 = (s32[1024]{0:T(1024)S(1)}, s32[1024]{0:T(1024)}, u32[]{:S(2)}) copy-start(s32[1024]{0:T(1024)} %param.10) | copy-start | bytes 12292
  42.7 11.9 %collective-permute-start.2 = (bf16[512,256]{1,0:T(8,128)(2,1)S(1)}, bf16[512,256]{1,0:T(8,128)(2,1)S(1)}, u32[]{:S(2)}, u32[]{:S(2)}) collective-permute-start(bf16[512,256]{1,0:T(8,128)(2,1)S(1)} %bitcast.23), channel_id=1, source_target_pairs={{3,0},{0,1},{1,2},{2,3},{7,4},{4,5},{5,6},{6,7},{11,8},{8,9},{9,10... | collective-permute-start | bytes 786440 | tf_op jit(solution)/shard_map/ppermute | solution.py:230
  43.9 14.2 %collective-permute-start.1 = (bf16[512,256]{1,0:T(8,128)(2,1)S(1)}, bf16[512,256]{1,0:T(8,128)(2,1)S(1)}, u32[]{:S(2)}, u32[]{:S(2)}) collective-permute-start(bf16[512,256]{1,0:T(8,128)(2,1)S(1)} %bitcast.24), channel_id=1, source_target_pairs={{2,0},{3,1},{0,2},{1,3},{6,4},{7,5},{4,6},{5,7},{10,8},{11,9},{8,1... | collective-permute-start | bytes 786440 | tf_op jit(solution)/shard_map/ppermute | solution.py:230
  46.3 11.7 %collective-permute-start = (bf16[512,256]{1,0:T(8,128)(2,1)S(1)}, bf16[512,256]{1,0:T(8,128)(2,1)S(1)}, u32[]{:S(2)}, u32[]{:S(2)}) collective-permute-start(bf16[512,256]{1,0:T(8,128)(2,1)S(1)} %bitcast.25), channel_id=1, source_target_pairs={{1,0},{2,1},{3,2},{0,3},{5,4},{6,5},{7,6},{4,7},{9,8},{10,9},{11,1... | collective-permute-start | bytes 786440 | tf_op jit(solution)/shard_map/ppermute | solution.py:230
  47.5 0.7 copy-start.6
  54.6 3.5 %copy-start.3 = (s32[1024]{0:T(1024)S(1)}, s32[1024]{0:T(1024)}, u32[]{:S(2)}) copy-start(s32[1024]{0:T(1024)} %param.12) | copy-start | bytes 12292
  62.1 11.0 %collective-permute-start.3 = (bf16[512,256]{1,0:T(8,128)(2,1)S(1)}, bf16[512,256]{1,0:T(8,128)(2,1)S(1)}, u32[]{:S(2)}, u32[]{:S(2)}) collective-permute-start(bf16[512,256]{1,0:T(8,128)(2,1)S(1)} %get-tuple-element.23), channel_id=1, source_target_pairs={{3,0},{0,1},{1,2},{2,3},{7,4},{4,5},{5,6},{6,7},{11,8},{8,9},{9,10... | collective-permute-start | bytes 786440 | tf_op jit(solution)/shard_map/ppermute | solution.py:230
  63.2 14.3 %collective-permute-start.4 = (bf16[512,256]{1,0:T(8,128)(2,1)S(1)}, bf16[512,256]{1,0:T(8,128)(2,1)S(1)}, u32[]{:S(2)}, u32[]{:S(2)}) collective-permute-start(bf16[512,256]{1,0:T(8,128)(2,1)S(1)} %get-tuple-element.24), channel_id=1, source_target_pairs={{2,0},{3,1},{0,2},{1,3},{6,4},{7,5},{4,6},{5,7},{10,8},{11,9},{8,1... | collective-permute-start | bytes 786440 | tf_op jit(solution)/shard_map/ppermute | solution.py:230
  65.9 11.5 %collective-permute-start.5 = (bf16[512,256]{1,0:T(8,128)(2,1)S(1)}, bf16[512,256]{1,0:T(8,128)(2,1)S(1)}, u32[]{:S(2)}, u32[]{:S(2)}) collective-permute-start(bf16[512,256]{1,0:T(8,128)(2,1)S(1)} %get-tuple-element.25), channel_id=1, source_target_pairs={{1,0},{2,1},{3,2},{0,3},{5,4},{6,5},{7,6},{4,7},{9,8},{10,9},{11,1... | collective-permute-start | bytes 786440 | tf_op jit(solution)/shard_map/ppermute | solution.py:230
  78.4 20.8 %all-to-all-start.2 = ((bf16[64,8,384]{2,1,0:T(8,128)(2,1)}), bf16[64,8,384]{2,1,0:T(8,128)(2,1)S(1)}, u32[]{:S(2)}, u32[]{:S(2)}) async-start(bf16[64,8,384]{2,1,0:T(8,128)(2,1)} %maximum_bitcast_fusion), calls=%async_computation.2 | async-start | bytes 786432 | tf_op jit(solution)/shard_map/all_to_all | solution.py:341
  100.2 10.7 %collective-permute-start.6 = (bf16[256,256]{1,0:T(8,128)(2,1)S(1)}, bf16[256,256]{1,0:T(8,128)(2,1)S(1)}, u32[]{:S(2)}, u32[]{:S(2)}) collective-permute-start(bf16[256,256]{1,0:T(8,128)(2,1)S(1)} %get-tuple-element.33), channel_id=1, source_target_pairs={{3,0},{0,1},{1,2},{2,3},{7,4},{4,5},{5,6},{6,7},{11,8},{8,9},{9,10... | collective-permute-start | bytes 393224 | tf_op jit(solution)/shard_map/ppermute | solution.py:230
  101.1 9.8 %collective-permute-start.7 = (bf16[256,256]{1,0:T(8,128)(2,1)S(1)}, bf16[256,256]{1,0:T(8,128)(2,1)S(1)}, u32[]{:S(2)}, u32[]{:S(2)}) collective-permute-start(bf16[256,256]{1,0:T(8,128)(2,1)S(1)} %get-tuple-element.34), channel_id=1, source_target_pairs={{2,0},{3,1},{0,2},{1,3},{6,4},{7,5},{4,6},{5,7},{10,8},{11,9},{8,1... | collective-permute-start | bytes 393224 | tf_op jit(solution)/shard_map/ppermute | solution.py:230
  103.3 7.6 %collective-permute-start.8 = (bf16[256,256]{1,0:T(8,128)(2,1)S(1)}, bf16[256,256]{1,0:T(8,128)(2,1)S(1)}, u32[]{:S(2)}, u32[]{:S(2)}) collective-permute-start(bf16[256,256]{1,0:T(8,128)(2,1)S(1)} %get-tuple-element.35), channel_id=1, source_target_pairs={{1,0},{2,1},{3,2},{0,3},{5,4},{6,5},{7,6},{4,7},{9,8},{10,9},{11,1... | collective-permute-start | bytes 393224 | tf_op jit(solution)/shard_map/ppermute | solution.py:230
  104.6 17.4 %all-to-all-start.3 = ((bf16[64,8,128]{2,1,0:T(8,128)(2,1)}), bf16[64,8,128]{2,1,0:T(8,128)(2,1)S(1)}, u32[]{:S(2)}, u32[]{:S(2)}) async-start(bf16[64,8,128]{2,1,0:T(8,128)(2,1)} %broadcast_in_dim.2), calls=%async_computation.3 | async-start | bytes 262144 | tf_op jit(solution)/shard_map/all_to_all | solution.py:344
  111.0 5.9 %collective-permute-start.11 = (bf16[256,256]{1,0:T(8,128)(2,1)S(1)}, bf16[256,256]{1,0:T(8,128)(2,1)S(1)}, u32[]{:S(2)}, u32[]{:S(2)}) collective-permute-start(bf16[256,256]{1,0:T(8,128)(2,1)S(1)} %add_convert_fusion.1.refs_0_), channel_id=1, source_target_pairs={{3,0},{0,1},{1,2},{2,3},{7,4},{4,5},{5,6},{6,7},{11,8},{8,9},{9,10... | collective-permute-start | bytes 393224 | tf_op jit(solution)/shard_map/ppermute | solution.py:230
  112.0 7.9 %collective-permute-start.10 = (bf16[256,256]{1,0:T(8,128)(2,1)S(1)}, bf16[256,256]{1,0:T(8,128)(2,1)S(1)}, u32[]{:S(2)}, u32[]{:S(2)}) collective-permute-start(bf16[256,256]{1,0:T(8,128)(2,1)S(1)} %add_convert_fusion.1.refs_0_), channel_id=1, source_target_pairs={{2,0},{3,1},{0,2},{1,3},{6,4},{7,5},{4,6},{5,7},{10,8},{11,9},{8,1... | collective-permute-start | bytes 393224 | tf_op jit(solution)/shard_map/ppermute | solution.py:230
  114.0 6.0 %collective-permute-start.9 = (bf16[256,256]{1,0:T(8,128)(2,1)S(1)}, bf16[256,256]{1,0:T(8,128)(2,1)S(1)}, u32[]{:S(2)}, u32[]{:S(2)}) collective-permute-start(bf16[256,256]{1,0:T(8,128)(2,1)S(1)} %add_convert_fusion.1.refs_0_), channel_id=1, source_target_pairs={{1,0},{2,1},{3,2},{0,3},{5,4},{6,5},{7,6},{4,7},{9,8},{10,9},{11,1... | collective-permute-start | bytes 393224 | tf_op jit(solution)/shard_map/ppermute | solution.py:230

commit v5 on v4

--- a/solution.py
+++ b/solution.py
@@ -9,7 +9,7 @@
 
 F32 = jnp.float32
 BF16 = jnp.bfloat16
-TILE = 512
+TILE = 1024
 SMEM = pl.BlockSpec(memory_space=pltpu.SMEM)
 ANY = pl.BlockSpec(memory_space=pl.ANY)
 CONTRACT_LAST = (((1,), (1,)), ((), ()))
@@ -156,9 +156,8 @@
     @pl.when(step == pl.num_programs(0) - 1)
     def _():
         for c in range(n_rel):
-            for k in range(rows // TILE):
-                hot = hot_columns(places[...] - (c * rows + k * TILE), TILE)
-                outs[c][k * TILE : (k + 1) * TILE, :] = dot(hot, weighted[...]).astype(BF16)
+            hot = hot_columns(places[...] - c * rows, rows)
+            outs[c][...] = dot(hot, weighted[...]).astype(BF16)
 
 
 def grad_kernel(

time: 124 us -> 125 us (level)
  waiting for transfers between devices: 35.5 us -> 37.1 us
    ppermute x12, waiting for transfers between devices: 13.3 us -> 14.8 us  [ring(): lax.ppermute(x, 'rel', [((k + shift) % n_rel, k) for k in range(n_rel)])]
    pallas_call x1, Pallas kernels: 3.96 us -> 5.4 us  [local(): pl.pallas_call(functools.partial(tail_kernel, n_rel, share), grid=(steps,...]
    pallas_call x1, Pallas kernels: 6.4 us -> 5.07 us  [local(): pl.pallas_call(functools.partial(head_kernel, r_count, blocks), grid=(ste...]
  transfers between devices with their start and end apart: 15 -> 15, of which waited for: 8 -> 8; matrix products, arithmetic and copies ran while one was open for 1% -> 1% of each run, Pallas kernels for 13% -> 11%
where the time goes in v5:
time: 125 us
  starting transfers between devices  41.4 us (33%)
  waiting for transfers between devices  37.1 us (30%)
  Pallas kernels  22.6 us (18%)
  blocking collectives  17.1 us (14%)
  local copies, waits for them, and re-layouts  3.81 us (3%)
  between operations  1.43 us (1%)
    all_to_all x1, blocking collectives, local(): fetched = lax.all_to_all(picked, 'ent', 0, 0, tiled=True)  17.1 us
    ppermute x12, starting transfers between devices, ring(): lax.ppermute(x, 'rel', [((k + shift) % n_rel, k) for k in range(n_rel)])  16.3 us
    ppermute x12, waiting for transfers between devices, ring(): lax.ppermute(x, 'rel', [((k + shift) % n_rel, k) for k in range(n_rel)])  14.8 us
    all_to_all x1, waiting for transfers between devices, local(): returned = lax.all_to_all(packed, 'ent', 0, 0, tiled=True)  14.3 us
    all_to_all x1, starting transfers between devices, local(): lax.all_to_all(request_rows.reshape(parts, 1, slots), 'ent', 0, 0, tiled=...  13.1 us
    all_to_all x1, waiting for transfers between devices, local(): lax.all_to_all(request_rows.reshape(parts, 1, slots), 'ent', 0, 0, tiled=...  7.52 us
    pallas_call x1, Pallas kernels, local(): pl.pallas_call(functools.partial(grad_kernel, blocks), grid=(r_count,), i...  6.51 us
    all_to_all x1, starting transfers between devices, local(): rel_all = lax.all_to_all(rel_all, 'ent', 0, 0, tiled=True)  6.31 us
  transfers between devices with their start and end apart: 15, of which 8 were waited for; matrix products, arithmetic and copies ran while one was open for 1% of the time, Pallas kernels for 11%

profile of v5, /device:TPU:1, one launch (start us, length us, event | category | flops | bytes accessed | tf_op | source)
XLA Modules:
  0.0 124.6 jit_solution(3075593584416549818)
XLA Ops:
  0.6 1.4 %copy.11 = s32[1,64,32]{2,1,0:T(8,128)} copy(s32[1,64,32]{1,2,0:T(8,128)} %param.9) | data formatting | bytes 16384 | tf_op args[1]
  2.0 13.1 %all-to-all-start = ((s32[64,1,32]{2,1,0:T(1,128)}), s32[64,1,32]{2,1,0:T(1,128)S(1)}, u32[]{:S(2)}, u32[]{:S(2)}) async-start(s32[64,1,32]{2,1,0:T(1,128)} %bitcast.6), calls=%async_computation | async-start | bytes 65536 | tf_op jit(solution)/shard_map/all_to_all | solution.py:248
  17.0 7.5 %all-to-all-done = s32[64,1,32]{2,1,0:T(1,128)S(1)} async-done(((s32[64,1,32]{2,1,0:T(1,128)}), s32[64,1,32]{2,1,0:T(1,128)S(1)}, u32[]{:S(2)}, u32[]{:S(2)}) %all-to-all-start) | async-done | bytes 8224 | tf_op jit(solution)/shard_map/all_to_all | solution.py:248
  24.5 1.1 pick.1
  25.6 17.1 %all_to_all.36 = bf16[64,8,256]{2,1,0:T(8,128)(2,1)S(1)} all-to-all(bf16[64,8,256]{2,1,0:T(8,128)(2,1)S(1)} %bitcast.27), channel_id=1, replica_groups=mesh['ent'=64,'rel'=4] {'ent'}, dimensions={0} | all-to-all | bytes 524288 | tf_op jit(solution)/shard_map/all_to_all | solution.py:297
  42.7 1.2 collective-permute-start.2
  43.9 2.5 %collective-permute-start.1 = (bf16[512,256]{1,0:T(8,128)(2,1)S(1)}, bf16[512,256]{1,0:T(8,128)(2,1)S(1)}, u32[]{:S(2)}, u32[]{:S(2)}) collective-permute-start(bf16[512,256]{1,0:T(8,128)(2,1)S(1)} %bitcast.24), channel_id=1, source_target_pairs={{2,0},{3,1},{0,2},{1,3},{6,4},{7,5},{4,6},{5,7},{10,8},{11,9},{8,1... | collective-permute-start | bytes 786440 | tf_op jit(solution)/shard_map/ppermute | solution.py:229
  46.3 1.2 collective-permute-start
  48.2 5.1 %head_step.1 = (bf16[1024,256]{1,0:T(8,128)(2,1)S(1)}, f32[1024,256]{1,0:T(8,128)S(1)}, bf16[256,1024]{1,0:T(8,128)(2,1)S(1)}, f32[1024,256]{1,0:T(8,128)S(1)}, bf16[2048,256]{1,0:T(8,128)(2,1)S(1)}) custom-call(s32[2]{0:T(128)S(1)} %pad_add_fusion.scal, s32[1,1,1024]{2,1,0:T(1,128)S(1)} %bitcast.32, s32[1,1,1024]{2,1,0:T(1,128)S(1)} %bitcast.34, ...), custom_call_target="tpu_custom_call" | custom-call | flops 3000000000 | bytes 6000000 | tf_op jit(solution)/shard_map/head_step/pallas_call | solution.py:276
  53.3 4.8 %collective-permute-done.1.refs_2_ = bf16[512,256]{1,0:T(8,128)(2,1)S(1)} collective-permute-done((bf16[512,256]{1,0:T(8,128)(2,1)S(1)}, bf16[512,256]{1,0:T(8,128)(2,1)S(1)}, u32[]{:S(2)}, u32[]{:S(2)}) %collective-permute-start.1) | collective-permute-done | bytes 262176 | tf_op jit(solution)/shard_map/ppermute | solution.py:229
  58.1 5.4 %tail_step.1 = (bf16[1024,256]{1,0:T(8,128)(2,1)S(1)}, bf16[512,256]{1,0:T(8,128)(2,1)S(1)}, bf16[512,256]{1,0:T(8,128)(2,1)S(1)}, bf16[512,256]{1,0:T(8,128)(2,1)S(1)}, bf16[512,256]{1,0:T(8,128)(2,1)S(1)}) custom-call(s32[2]{0:T(128)S(1)} %pad_add_fusion.scal, s32[1,1,1024]{2,1,0:T(1,128)S(1)} %bitcast.31, bf16[1024,256]{1,0:T(8,128)(2,1)S(1)} %get-tuple-element.20.proj, ...), custom_call_target="tpu_custom_call" | custom-call | flops 3000000000 | bytes 5000000 | tf_op jit(solution)/shard_map/tail_step/pallas_call | solution.py:300
  63.5 1.1 collective-permute-start.3
  64.6 2.8 %collective-permute-start.4 = (bf16[512,256]{1,0:T(8,128)(2,1)S(1)}, bf16[512,256]{1,0:T(8,128)(2,1)S(1)}, u32[]{:S(2)}, u32[]{:S(2)}) collective-permute-start(bf16[512,256]{1,0:T(8,128)(2,1)S(1)} %get-tuple-element.24), channel_id=1, source_target_pairs={{2,0},{3,1},{0,2},{1,3},{6,4},{7,5},{4,6},{5,7},{10,8},{11,9},{8,1... | collective-permute-start | bytes 786440 | tf_op jit(solution)/shard_map/ppermute | solution.py:229
  67.8 6.5 %grad_step.1 = (bf16[512,128]{1,0:T(8,128)(2,1)S(1)}, f32[1024,256]{1,0:T(8,128)S(1)}) custom-call(s32[1,1024]{1,0:T(1,128)S(1)} %bitcast.33, s32[1,1024]{1,0:T(1,128)S(1)} %bitcast.35, bf16[1024,256]{1,0:T(8,128)(2,1)S(1)} %get-tuple-element.26.gp.after, bf16[256,1024]{1,0:T(8,128)(2,1)S(1)} %get-tuple-element.27.turned, ...), custom_call_target="tpu_custom_call" | custom-call | flops 3000000000 | bytes 6000000 | tf_op jit(solution)/shard_map/grad_step/pallas_call | solution.py:324
  74.3 4.6 %collective-permute-done.4 = bf16[512,256]{1,0:T(8,128)(2,1)S(1)} collective-permute-done((bf16[512,256]{1,0:T(8,128)(2,1)S(1)}, bf16[512,256]{1,0:T(8,128)(2,1)S(1)}, u32[]{:S(2)}, u32[]{:S(2)}) %collective-permute-start.4) | collective-permute-done | bytes 262176 | tf_op jit(solution)/shard_map/ppermute | solution.py:229
  79.8 5.6 %all-to-all-start.2 = ((bf16[64,8,384]{2,1,0:T(8,128)(2,1)}), bf16[64,8,384]{2,1,0:T(8,128)(2,1)S(1)}, u32[]{:S(2)}, u32[]{:S(2)}) async-start(bf16[64,8,384]{2,1,0:T(8,128)(2,1)} %maximum_bitcast_fusion), calls=%async_computation.2 | async-start | bytes 786432 | tf_op jit(solution)/shard_map/all_to_all | solution.py:340
  86.3 14.3 %all-to-all-done.2 = bf16[64,8,384]{2,1,0:T(8,128)(2,1)S(1)} async-done(((bf16[64,8,384]{2,1,0:T(8,128)(2,1)}), bf16[64,8,384]{2,1,0:T(8,128)(2,1)S(1)}, u32[]{:S(2)}, u32[]{:S(2)}) %all-to-all-start.2) | async-done | bytes 393248 | tf_op jit(solution)/shard_map/all_to_all | solution.py:340
  102.6 2.2 %collective-permute-start.7 = (bf16[256,256]{1,0:T(8,128)(2,1)S(1)}, bf16[256,256]{1,0:T(8,128)(2,1)S(1)}, u32[]{:S(2)}, u32[]{:S(2)}) collective-permute-start(bf16[256,256]{1,0:T(8,128)(2,1)S(1)} %get-tuple-element.34), channel_id=1, source_target_pairs={{2,0},{3,1},{0,2},{1,3},{6,4},{7,5},{4,6},{5,7},{10,8},{11,9},{8,1... | collective-permute-start | bytes 393224 | tf_op jit(solution)/shard_map/ppermute | solution.py:229
  106.0 6.3 %all-to-all-start.3 = ((bf16[64,8,128]{2,1,0:T(8,128)(2,1)}), bf16[64,8,128]{2,1,0:T(8,128)(2,1)S(1)}, u32[]{:S(2)}, u32[]{:S(2)}) async-start(bf16[64,8,128]{2,1,0:T(8,128)(2,1)} %broadcast_in_dim.2), calls=%async_computation.3 | async-start | bytes 262144 | tf_op jit(solution)/shard_map/all_to_all | solution.py:343
  113.5 2.0 %collective-permute-start.10 = (bf16[256,256]{1,0:T(8,128)(2,1)S(1)}, bf16[256,256]{1,0:T(8,128)(2,1)S(1)}, u32[]{:S(2)}, u32[]{:S(2)}) collective-permute-start(bf16[256,256]{1,0:T(8,128)(2,1)S(1)} %add_convert_fusion.1.refs_0_), channel_id=1, source_target_pairs={{2,0},{3,1},{0,2},{1,3},{6,4},{7,5},{4,6},{5,7},{10,8},{11,9},{8,1... | collective-permute-start | bytes 393224 | tf_op jit(solution)/shard_map/ppermute | solution.py:229
  116.0 2.3 %collective-permute-done.11.refs_3_ = bf16[256,256]{1,0:T(8,128)(2,1)S(1)} collective-permute-done((bf16[256,256]{1,0:T(8,128)(2,1)S(1)}, bf16[256,256]{1,0:T(8,128)(2,1)S(1)}, u32[]{:S(2)}, u32[]{:S(2)}) %collective-permute-start.11) | collective-permute-done | bytes 131104 | tf_op jit(solution)/shard_map/ppermute | solution.py:229
  118.3 3.0 %collective-permute-done.10.refs_2_ = bf16[256,256]{1,0:T(8,128)(2,1)S(1)} collective-permute-done((bf16[256,256]{1,0:T(8,128)(2,1)S(1)}, bf16[256,256]{1,0:T(8,128)(2,1)S(1)}, u32[]{:S(2)}, u32[]{:S(2)}) %collective-permute-start.10) | collective-permute-done | bytes 131104 | tf_op jit(solution)/shard_map/ppermute | solution.py:229
  121.5 1.6 %place_rows.1 = f32[1024,256]{1,0:T(8,128)} custom-call(s32[2]{0:T(128)S(1)} %pad_add_fusion.scal, bf16[256,256]{1,0:T(8,128)(2,1)S(1)} %add_convert_fusion.1.refs_0_, bf16[256,256]{1,0:T(8,128)(2,1)S(1)} %collective-permute-done.9.refs_1_, bf16[256,256]{1,0:T(8,128)(2,1)S(1)} %collective-permute-done.10.refs_2_, ...), custom_call_target="tpu_custom_call" | custom-call | flops 1000000 | bytes 1500000 | tf_op jit(solution)/shard_map/place_rows/pallas_call | solution.py:359
  123.4 1.1 relation_out.1
  (37 shorter events, 9.4 us)
Async XLA Ops:
  2.0 22.5 %all-to-all-start = ((s32[64,1,32]{2,1,0:T(1,128)}), s32[64,1,32]{2,1,0:T(1,128)S(1)}, u32[]{:S(2)}, u32[]{:S(2)}) async-start(s32[64,1,32]{2,1,0:T(1,128)} %bitcast.6), calls=%async_computation | async-start | bytes 65536 | tf_op jit(solution)/shard_map/all_to_all | solution.py:248
  15.9 1.0 copy-start
  24.5 23.0 %copy-start.1 = (bf16[1024,256]{1,0:T(8,128)(2,1)S(1)}, bf16[1024,256]{1,0:T(8,128)(2,1)}, u32[]{:S(2)}) copy-start(bf16[1024,256]{1,0:T(8,128)(2,1)} %table.3) | copy-start | bytes 1572868
  24.5 23.0 %copy-start.2 = (bf16[8,8,32,32]{3,2,1,0:T(8,128)(2,1)S(1)}, bf16[8,8,32,32]{3,2,1,0:T(8,128)(2,1)}, u32[]{:S(2)}) copy-start(bf16[8,8,32,32]{3,2,1,0:T(8,128)(2,1)} %param.15) | copy-start | bytes 393220
  42.7 4.8 %copy-start.5 = (s32[1024]{0:T(1024)S(1)}, s32[1024]{0:T(1024)}, u32[]{:S(2)}) copy-start(s32[1024]{0:T(1024)} %param.11) | copy-start | bytes 12292
  42.7 4.8 %copy-start.4 = (s32[1024]{0:T(1024)S(1)}, s32[1024]{0:T(1024)}, u32[]{:S(2)}) copy-start(s32[1024]{0:T(1024)} %param.10) | copy-start | bytes 12292
  42.7 10.6 %collective-permute-start.2 = (bf16[512,256]{1,0:T(8,128)(2,1)S(1)}, bf16[512,256]{1,0:T(8,128)(2,1)S(1)}, u32[]{:S(2)}, u32[]{:S(2)}) collective-permute-start(bf16[512,256]{1,0:T(8,128)(2,1)S(1)} %bitcast.23), channel_id=1, source_target_pairs={{3,0},{0,1},{1,2},{2,3},{7,4},{4,5},{5,6},{6,7},{11,8},{8,9},{9,10... | collective-permute-start | bytes 786440 | tf_op jit(solution)/shard_map/ppermute | solution.py:229
  43.9 14.2 %collective-permute-start.1 = (bf16[512,256]{1,0:T(8,128)(2,1)S(1)}, bf16[512,256]{1,0:T(8,128)(2,1)S(1)}, u32[]{:S(2)}, u32[]{:S(2)}) collective-permute-start(bf16[512,256]{1,0:T(8,128)(2,1)S(1)} %bitcast.24), channel_id=1, source_target_pairs={{2,0},{3,1},{0,2},{1,3},{6,4},{7,5},{4,6},{5,7},{10,8},{11,9},{8,1... | collective-permute-start | bytes 786440 | tf_op jit(solution)/shard_map/ppermute | solution.py:229
  46.3 11.7 %collective-permute-start = (bf16[512,256]{1,0:T(8,128)(2,1)S(1)}, bf16[512,256]{1,0:T(8,128)(2,1)S(1)}, u32[]{:S(2)}, u32[]{:S(2)}) collective-permute-start(bf16[512,256]{1,0:T(8,128)(2,1)S(1)} %bitcast.25), channel_id=1, source_target_pairs={{1,0},{2,1},{3,2},{0,3},{5,4},{6,5},{7,6},{4,7},{9,8},{10,9},{11,1... | collective-permute-start | bytes 786440 | tf_op jit(solution)/shard_map/ppermute | solution.py:229
  47.5 0.7 copy-start.6
  53.3 4.8 %copy-start.3 = (s32[1024]{0:T(1024)S(1)}, s32[1024]{0:T(1024)}, u32[]{:S(2)}) copy-start(s32[1024]{0:T(1024)} %param.12) | copy-start | bytes 12292
  63.5 10.8 %collective-permute-start.3 = (bf16[512,256]{1,0:T(8,128)(2,1)S(1)}, bf16[512,256]{1,0:T(8,128)(2,1)S(1)}, u32[]{:S(2)}, u32[]{:S(2)}) collective-permute-start(bf16[512,256]{1,0:T(8,128)(2,1)S(1)} %get-tuple-element.23), channel_id=1, source_target_pairs={{3,0},{0,1},{1,2},{2,3},{7,4},{4,5},{5,6},{6,7},{11,8},{8,9},{9,10... | collective-permute-start | bytes 786440 | tf_op jit(solution)/shard_map/ppermute | solution.py:229
  64.6 14.3 %collective-permute-start.4 = (bf16[512,256]{1,0:T(8,128)(2,1)S(1)}, bf16[512,256]{1,0:T(8,128)(2,1)S(1)}, u32[]{:S(2)}, u32[]{:S(2)}) collective-permute-start(bf16[512,256]{1,0:T(8,128)(2,1)S(1)} %get-tuple-element.24), channel_id=1, source_target_pairs={{2,0},{3,1},{0,2},{1,3},{6,4},{7,5},{4,6},{5,7},{10,8},{11,9},{8,1... | collective-permute-start | bytes 786440 | tf_op jit(solution)/shard_map/ppermute | solution.py:229
  67.4 11.5 %collective-permute-start.5 = (bf16[512,256]{1,0:T(8,128)(2,1)S(1)}, bf16[512,256]{1,0:T(8,128)(2,1)S(1)}, u32[]{:S(2)}, u32[]{:S(2)}) collective-permute-start(bf16[512,256]{1,0:T(8,128)(2,1)S(1)} %get-tuple-element.25), channel_id=1, source_target_pairs={{1,0},{2,1},{3,2},{0,3},{5,4},{6,5},{7,6},{4,7},{9,8},{10,9},{11,1... | collective-permute-start | bytes 786440 | tf_op jit(solution)/shard_map/ppermute | solution.py:229
  79.8 20.8 %all-to-all-start.2 = ((bf16[64,8,384]{2,1,0:T(8,128)(2,1)}), bf16[64,8,384]{2,1,0:T(8,128)(2,1)S(1)}, u32[]{:S(2)}, u32[]{:S(2)}) async-start(bf16[64,8,384]{2,1,0:T(8,128)(2,1)} %maximum_bitcast_fusion), calls=%async_computation.2 | async-start | bytes 786432 | tf_op jit(solution)/shard_map/all_to_all | solution.py:340
  101.6 10.7 %collective-permute-start.6 = (bf16[256,256]{1,0:T(8,128)(2,1)S(1)}, bf16[256,256]{1,0:T(8,128)(2,1)S(1)}, u32[]{:S(2)}, u32[]{:S(2)}) collective-permute-start(bf16[256,256]{1,0:T(8,128)(2,1)S(1)} %get-tuple-element.33), channel_id=1, source_target_pairs={{3,0},{0,1},{1,2},{2,3},{7,4},{4,5},{5,6},{6,7},{11,8},{8,9},{9,10... | collective-permute-start | bytes 393224 | tf_op jit(solution)/shard_map/ppermute | solution.py:229
  102.6 9.8 %collective-permute-start.7 = (bf16[256,256]{1,0:T(8,128)(2,1)S(1)}, bf16[256,256]{1,0:T(8,128)(2,1)S(1)}, u32[]{:S(2)}, u32[]{:S(2)}) collective-permute-start(bf16[256,256]{1,0:T(8,128)(2,1)S(1)} %get-tuple-element.34), channel_id=1, source_target_pairs={{2,0},{3,1},{0,2},{1,3},{6,4},{7,5},{4,6},{5,7},{10,8},{11,9},{8,1... | collective-permute-start | bytes 393224 | tf_op jit(solution)/shard_map/ppermute | solution.py:229
  104.8 7.6 %collective-permute-start.8 = (bf16[256,256]{1,0:T(8,128)(2,1)S(1)}, bf16[256,256]{1,0:T(8,128)(2,1)S(1)}, u32[]{:S(2)}, u32[]{:S(2)}) collective-permute-start(bf16[256,256]{1,0:T(8,128)(2,1)S(1)} %get-tuple-element.35), channel_id=1, source_target_pairs={{1,0},{2,1},{3,2},{0,3},{5,4},{6,5},{7,6},{4,7},{9,8},{10,9},{11,1... | collective-permute-start | bytes 393224 | tf_op jit(solution)/shard_map/ppermute | solution.py:229
  106.0 17.4 %all-to-all-start.3 = ((bf16[64,8,128]{2,1,0:T(8,128)(2,1)}), bf16[64,8,128]{2,1,0:T(8,128)(2,1)S(1)}, u32[]{:S(2)}, u32[]{:S(2)}) async-start(bf16[64,8,128]{2,1,0:T(8,128)(2,1)} %broadcast_in_dim.2), calls=%async_computation.3 | async-start | bytes 262144 | tf_op jit(solution)/shard_map/all_to_all | solution.py:343
  112.5 5.9 %collective-permute-start.11 = (bf16[256,256]{1,0:T(8,128)(2,1)S(1)}, bf16[256,256]{1,0:T(8,128)(2,1)S(1)}, u32[]{:S(2)}, u32[]{:S(2)}) collective-permute-start(bf16[256,256]{1,0:T(8,128)(2,1)S(1)} %add_convert_fusion.1.refs_0_), channel_id=1, source_target_pairs={{3,0},{0,1},{1,2},{2,3},{7,4},{4,5},{5,6},{6,7},{11,8},{8,9},{9,10... | collective-permute-start | bytes 393224 | tf_op jit(solution)/shard_map/ppermute | solution.py:229
  113.5 7.9 %collective-permute-start.10 = (bf16[256,256]{1,0:T(8,128)(2,1)S(1)}, bf16[256,256]{1,0:T(8,128)(2,1)S(1)}, u32[]{:S(2)}, u32[]{:S(2)}) collective-permute-start(bf16[256,256]{1,0:T(8,128)(2,1)S(1)} %add_convert_fusion.1.refs_0_), channel_id=1, source_target_pairs={{2,0},{3,1},{0,2},{1,3},{6,4},{7,5},{4,6},{5,7},{10,8},{11,9},{8,1... | collective-permute-start | bytes 393224 | tf_op jit(solution)/shard_map/ppermute | solution.py:229
  115.4 6.0 %collective-permute-start.9 = (bf16[256,256]{1,0:T(8,128)(2,1)S(1)}, bf16[256,256]{1,0:T(8,128)(2,1)S(1)}, u32[]{:S(2)}, u32[]{:S(2)}) collective-permute-start(bf16[256,256]{1,0:T(8,128)(2,1)S(1)} %add_convert_fusion.1.refs_0_), channel_id=1, source_target_pairs={{1,0},{2,1},{3,2},{0,3},{5,4},{6,5},{7,6},{4,7},{9,8},{10,9},{11,1... | collective-permute-start | bytes 393224 | tf_op jit(solution)/shard_map/ppermute | solution.py:229
